TPU v7x, 256 devices: a whole 4x4x8 slice. The times are simulated.
256 devices in a mesh: rows: 64 (over z_hi, y, x, core), lags: 4 (over z_lo).
Axes of the slice: x: 4, y: 4, z: 8 (z_hi: 2, z_lo: 4; z = z_hi * 4 + z_lo), core: 2. Of those that a mesh axis runs over, the one named last changes fastest.
Arguments:
- history: float32 [32, 16, 16384], P('lags', None, 'rows'), may hold values from -6 to 6
- incident: float32 [2, 16, 16384], P(None, None, 'rows'), may hold values from -6 to 6
- kernel: float32 [64, 32, 6, 256, 256], P('rows', 'lags'), may hold values from -0.02734375 to 0.02734375
- near_blocks: int32 [64, 32, 6], P('rows', 'lags'), may hold values from 0 to 63, as said below
- self_inverse: float32 [64, 256, 256], P('rows'), may hold values from -1 to 1
Outputs:
- densities: float32 [2, 16, 16384], P(None, None, 'rows')
Inputs may be any that keep to these rules, and one draw needn't show every extreme that they name: `near_blocks`: indices of source blocks; for each row block and each group of 8 consecutive lags, no source block appears more than 1 times among its 48 entries, and some block appears exactly 1 times.
All inputs are finite; a program needn't handle non-finite values.
Results may differ from a plain program's by a relative error of at most 0.00012.
Values sent between devices are 32-bit elements; how exact they have to be, the bound alone decides.
No kernel may reach another device: no remote copies, remote signals or barrier semaphores. Data moves between devices by JAX's collectives and lax.ppermute only.
A program may use at most 128 MiB of HBM per device.

v0:
```python
import jax
import jax.numpy as jnp
from jax import lax
from jax.sharding import PartitionSpec as P


def shifted(block, axis, distance):
    devices = range(lax.axis_size(axis))
    route = [(i - distance, i) for i in devices if i - distance in devices]
    return lax.ppermute(block, axis, route)


def shards(history, incident, kernel, near_blocks, self_inverse):
    highest = lax.Precision.HIGHEST
    lag_dev, wave_count, block_size = history.shape
    step_count = incident.shape[0]
    lag_group = lax.axis_index("lags")
    kernel_rows = kernel[0]
    source_ids = near_blocks[0]
    inverse = self_inverse[0]
    lag_ids = jnp.arange(lag_dev, dtype=jnp.int32)

    def solve_from(instant, picked):
        partial_value = jnp.einsum("jkwc,jkcr->wr", picked, kernel_rows, precision=highest)
        driving = lax.dynamic_index_in_dim(incident, instant, 0, keepdims=False)
        near_field = lax.psum(partial_value, "lags")
        result = jnp.dot(
            driving - near_field, inverse, precision=highest, preferred_element_type=jnp.float32
        )
        return result

    outputs = jnp.zeros((step_count, wave_count, block_size), jnp.float32)
    gathered = lax.all_gather(history, "rows", axis=2, tiled=True)
    block_total = gathered.shape[2] // block_size

    def density_at(instant, columns):
        slot_ids = jnp.remainder(lag_ids - instant, lag_dev)
        blocks = columns.reshape(lag_dev, wave_count, block_total, block_size)
        picked = blocks[slot_ids[:, None], :, source_ids]
        return solve_from(instant, picked)

    def advance(instant, state_tuple):
        columns, local_window, results = state_tuple
        density = density_at(instant, columns)
        results = lax.dynamic_update_index_in_dim(results, density, instant, 0)
        free_slot = jnp.remainder(lag_dev - 1 - instant, lag_dev)
        fresh_columns = lax.all_gather(density, "rows", axis=1, tiled=True)
        leaving = lax.dynamic_index_in_dim(columns, free_slot, 0, keepdims=False)
        passed = shifted(leaving, "lags", 1)
        entering = jnp.where(lag_group == 0, fresh_columns, passed)
        columns = lax.dynamic_update_index_in_dim(columns, entering, free_slot, 0)
        return (columns, local_window, results)

    gathered, local_window, outputs = lax.fori_loop(
        0, step_count - 1, advance, (gathered, history, outputs)
    )
    last_density = density_at(step_count - 1, gathered)
    outputs = lax.dynamic_update_index_in_dim(outputs, last_density, step_count - 1, 0)
    return outputs


def solution(mesh):
    in_specs = (
        P("lags", None, "rows"),
        P(None, None, "rows"),
        P("rows", "lags", None, None, None),
        P("rows", "lags", None),
        P("rows", None, None),
    )
    out_specs = P(None, None, "rows")
    return jax.shard_map(shards, mesh=mesh, in_specs=in_specs, out_specs=out_specs, check_vma=False)
```

profile of v0, /device:TPU:2, one launch (start us, length us, event | category | flops | bytes accessed | tf_op | source)
XLA Modules:
  0.0 291.4 jit_solution(5656090573350657618)
XLA Ops:
  6.5 0.0 copy-start
  6.5 0.0 all-gather.3.cloned.1.call-start
  6.5 0.7 all-gather.3.cloned.1.call-update
  7.3 0.0 all-gather.5.cloned.1.call-start
  7.3 0.7 broadcast_or_fusion
  8.1 0.1 copy.8
  8.1 0.1 reshape.79
  8.2 125.6 %all-gather.3.cloned.1.call-done = f32[8,16,16384]{2,1,0:T(8,128)} async-done(((f32[8,16,256]{2,1,0:T(8,128)}), f32[8,16,16384]{2,1,0:T(8,128)}) %all-gather.3.cloned.1.call-update) | async-done | bytes 8388624 | tf_op jit(solution)/shard_map/all_gather | solution.py:33
  133.8 7.8 %copy.19 = f32[8,2,64,8,256]{4,3,1,2,0:T(8,128)} copy(f32[8,2,64,8,256]{4,3,2,1,0:T(8,128)} %bitcast.54) | data formatting | bytes 16777216 | tf_op jit(solution)/shard_map/while/body/eval_jaxpr/reshape | solution.py:38
  141.6 0.0 copy-start.2
  141.6 4.2 %gather_fusion = f32[48,16,256]{2,1,0:T(8,128)S(1)} fusion(f32[8,16,64,256]{3,1,2,0:T(8,128)} %bitcast.57, s32[48]{0:T(128)S(1)} %reshape.79), kind=kCustom, calls=%fused_computation | custom fusion | bytes 1573248 | tf_op jit(solution)/shard_map/while/body/eval_jaxpr/gather | solution.py:39
  145.7 9.2 %fusion.4 = f32[16,256]{1,0:T(8,128)S(1)} fusion(f32[8,6,16,256]{3,2,1,0:T(8,128)S(1)} %bitcast.58, f32[1,8,6,256,256]{4,3,2,1,0:T(8,128)} %param.7), kind=kOutput, calls=%fused_computation.8 | convolution fusion | flops 603979776 | bytes 13385728 | tf_op jit(solution)/shard_map/while/body/eval_jaxpr/jkwc,jkcr->wr/dot_general | solution.py:24
  155.0 16.2 %psum.15 = f32[16,256]{1,0:T(8,128)S(1)} all-reduce(f32[16,256]{1,0:T(8,128)S(1)} %fusion.4), channel_id=1, replica_groups=mesh['rows'=64,'lags'=4] {'lags'}, use_global_device_ids=true, to_apply=%region_0.1 | all-reduce | flops 4096 | bytes 32768 | tf_op jit(solution)/shard_map/while/body/eval_jaxpr/psum | solution.py:26
  171.2 0.0 copy-done
  171.2 0.0 copy-done.2
  171.2 0.8 fusion.11
  172.1 0.0 all-gather.5.cloned.1.call-update
  172.1 1.3 slice_bitcast_fusion
  173.4 1.4 collective-permute-start
  174.8 0.1 copy.10
  174.8 0.1 reshape.85
  174.9 19.3 %collective-permute-done = f32[16,16384]{1,0:T(8,128)S(1)} collective-permute-done((f32[16,16384]{1,0:T(8,128)S(1)}, f32[16,16384]{1,0:T(8,128)S(1)}, u32[]{:S(2)}, u32[]{:S(2)}) %collective-permute-start) | collective-permute-done | bytes 1048608 | tf_op jit(solution)/shard_map/while/body/eval_jaxpr/ppermute | solution.py:10
  194.2 50.4 %all-gather.5.cloned.1.call-done = f32[16,16384]{1,0:T(8,128)} async-done(((f32[16,256]{1,0:T(8,128)}), f32[16,16384]{1,0:T(8,128)}) %all-gather.5.cloned.1.call-update) | async-done | bytes 1048592 | tf_op jit(solution)/shard_map/while/body/eval_jaxpr/all_gather | solution.py:47
  244.6 2.4 bitcast_dynamic-update-slice_fusion
  247.0 7.8 %copy.18 = f32[8,2,64,8,256]{4,3,1,2,0:T(8,128)} copy(f32[8,2,64,8,256]{4,3,2,1,0:T(8,128)} %bitcast.55) | data formatting | bytes 16777216 | tf_op jit(solution)/shard_map/reshape | solution.py:38
  254.8 0.0 copy-start.1
  254.8 4.2 %gather_fusion.1 = f32[48,16,256]{2,1,0:T(8,128)S(1)} fusion(f32[8,16,64,256]{3,1,2,0:T(8,128)} %bitcast.56, s32[48]{0:T(128)S(1)} %reshape.85), kind=kCustom, calls=%fused_computation.1 | custom fusion | bytes 1573248 | tf_op jit(solution)/shard_map/gather | solution.py:39
  259.0 9.2 %fusion.7 = f32[16,256]{1,0:T(8,128)S(1)} fusion(f32[8,6,16,256]{3,2,1,0:T(8,128)S(1)} %bitcast.59, f32[1,8,6,256,256]{4,3,2,1,0:T(8,128)} %param.7), kind=kOutput, calls=%fused_computation.9 | convolution fusion | flops 603979776 | bytes 13385728 | tf_op jit(solution)/shard_map/jkwc,jkcr->wr/dot_general | solution.py:24
  268.2 15.5 %psum.16 = f32[16,256]{1,0:T(8,128)S(1)} all-reduce(f32[16,256]{1,0:T(8,128)S(1)} %fusion.7), channel_id=1, replica_groups=mesh['rows'=64,'lags'=4] {'lags'}, use_global_device_ids=true, to_apply=%region_1.2 | all-reduce | flops 4096 | bytes 32768 | tf_op jit(solution)/shard_map/psum | solution.py:26
  283.7 0.2 convolution_bitcast_fusion
  283.9 0.0 copy-done.1
  284.0 0.6 pad_maximum_fusion
  (3 shorter events, 0.0 us)
Async XLA Ops:
  6.5 164.7 %copy-start = (f32[1,256,256]{2,1,0:T(8,128)S(1)}, f32[1,256,256]{2,1,0:T(8,128)}, u32[]{:S(2)}) copy-start(f32[1,256,256]{2,1,0:T(8,128)} %param.9) | copy-start | bytes 786436
  6.5 127.3 %all-gather.3.cloned.1.call-start = ((), (), s32[]{:S(2)}) async-start(), calls=%async_computation | async-start | bytes 8519680 | tf_op jit(solution)/shard_map/all_gather | solution.py:33
  7.3 237.3 %all-gather.5.cloned.1.call-start = ((), (), s32[]{:S(2)}) async-start(), calls=%async_computation.1 | async-start | bytes 1064960 | tf_op jit(solution)/shard_map/while/body/eval_jaxpr/all_gather | solution.py:47
  141.6 29.6 %copy-start.2 = (f32[2,16,256]{2,1,0:T(8,128)S(1)}, f32[2,16,256]{2,1,0:T(8,128)}, u32[]{:S(2)}) copy-start(f32[2,16,256]{2,1,0:T(8,128)} %param.6) | copy-start | bytes 98308
  173.4 20.9 %collective-permute-start = (f32[16,16384]{1,0:T(8,128)S(1)}, f32[16,16384]{1,0:T(8,128)S(1)}, u32[]{:S(2)}, u32[]{:S(2)}) collective-permute-start(f32[16,16384]{1,0:T(8,128)S(1)} %slice_bitcast_fusion), channel_id=1, source_target_pairs={{0,1},{1,2},{2,3},{4,5},{5,6},{6,7},{8,9},{9,10},{10,11},{12,13},{... | collective-permute-start | bytes 3145736 | tf_op jit(solution)/shard_map/while/body/eval_jaxpr/ppermute | solution.py:10
  254.8 29.2 %copy-start.1 = (f32[16,256]{1,0:T(8,128)S(1)}, f32[16,256]{1,0:T(8,128)}, u32[]{:S(2)}) copy-start(f32[16,256]{1,0:T(8,128)} %fusion.11) | copy-start | bytes 49156
Sparse Core Ops, SparseCore 0:
  10.7 123.0 all-gather.2
  172.2 72.3 all-gather.4
where the time goes:
time: 292 us; the launch traced here: 291 us
  waiting for transfers between devices  196 us (67%)
  blocking collectives  31.8 us (11%)
  local copies, waits for them, and re-layouts  25.5 us (9%)
  matrix products  19.5 us (7%)
  between operations  13.5 us (5%)
  other arithmetic  3.78 us (1%)
    all_gather x1, waiting for transfers between devices, shards(): gathered = lax.all_gather(history, 'rows', axis=2, tiled=True)  126 us
    all_gather x1, waiting for transfers between devices, advance(): fresh_columns = lax.all_gather(density, 'rows', axis=1, tiled=True)  50.4 us
    psum x2, blocking collectives, solve_from(): near_field = lax.psum(partial_value, 'lags')  31.8 us
    ppermute x1, waiting for transfers between devices, shifted(): return lax.ppermute(block, axis, route)  19.3 us
    dot_general x2, matrix products, solve_from(): jnp.einsum('jkwc,jkcr->wr', picked, kernel_rows, precision=highest)  18.4 us
    reshape x2, local copies, waits for them, and re-layouts, density_at(): blocks = columns.reshape(lag_dev, wave_count, block_total, block_size)  15.5 us
    gather x2, local copies, waits for them, and re-layouts, density_at(): picked = blocks[slot_ids[:, None], :, source_ids]  8.33 us
  transfers between devices with their start and end apart: 3, of which 3 were waited for; matrix products, arithmetic and copies ran while one was open for 1% of the time, Pallas kernels for 0%

commit v1 on v0

v1 whole, which is shorter than its diff:
```python
import jax
import jax.numpy as jnp
from jax import lax
from jax.experimental import pallas as pl
from jax.experimental.pallas import tpu as pltpu
from jax.sharding import Mesh
from jax.sharding import PartitionSpec as P

PLANE = ("y", "x", "core")
ROWS = ("z_hi",) + PLANE
F32 = jnp.float32
BF16 = jnp.bfloat16


def split(value):
    high = value.astype(BF16)
    low = (value - high.astype(F32)).astype(BF16)
    return high, low


def product(left, right):
    waves = left.shape[0]
    left_high, left_low = split(left)
    right_high, right_low = split(right)
    both = jnp.concatenate([left_high, left_low], axis=0)
    first = jnp.dot(both, right_high, preferred_element_type=F32)
    second = jnp.dot(left_high, right_low, preferred_element_type=F32)
    return first[:waves] + (first[waves:] + second)


def pack(table, own, twin, shift):
    peers, planes = table.shape
    block = own.shape[1:]

    def body(table_ref, own_ref, twin_ref, out_ref):
        for peer in range(peers):
            out_ref[peer, 0] = own_ref[table_ref[peer, 0] + shift]
            out_ref[peer, 1] = twin_ref[table_ref[peer, 1] + shift]

    vmem = pl.BlockSpec(memory_space=pltpu.VMEM)
    return pl.pallas_call(
        body,
        out_shape=jax.ShapeDtypeStruct((peers, planes) + block, F32),
        in_specs=[pl.BlockSpec(memory_space=pltpu.SMEM), vmem, vmem],
        out_specs=vmem,
        name=f"pack{shift}",
    )(table, own, twin)


def near_partial(ids, received, kernel, name):
    lag_dev, near, size, _ = kernel.shape
    peers, planes, waves, _ = received.shape

    def body(ids_ref, received_ref, kernel_ref, out_ref):
        lag = pl.program_id(0)
        total = jnp.zeros((waves, size), F32)
        for slot in range(near):
            source = ids_ref[lag, slot]
            block = received_ref[source % peers, source // peers]
            total = total + product(block, kernel_ref[0, slot])

        @pl.when(lag == 0)
        def _():
            out_ref[...] = total

        @pl.when(lag > 0)
        def _():
            out_ref[...] += total

    return pl.pallas_call(
        body,
        grid=(lag_dev,),
        out_shape=jax.ShapeDtypeStruct((waves, size), F32),
        in_specs=[
            pl.BlockSpec(memory_space=pltpu.SMEM),
            pl.BlockSpec(memory_space=pltpu.VMEM),
            pl.BlockSpec((1, near, size, size), lambda lag: (lag, 0, 0, 0)),
        ],
        out_specs=pl.BlockSpec((waves, size), lambda lag: (0, 0)),
        name=name,
    )(ids, received, kernel)


def first_density(plane, partials, incident, twin_incident, inverse, twin_inverse):
    groups = partials.shape[0] // 2
    waves, size = incident.shape

    def body(plane_ref, partials_ref, inc_ref, twin_inc_ref, inv_ref, twin_inv_ref, out_ref):
        own = plane_ref[0] * groups
        twin = groups - own
        near = partials_ref[own]
        twin_near = partials_ref[twin]
        for group in range(1, groups):
            near = near + partials_ref[own + group]
            twin_near = twin_near + partials_ref[twin + group]
        out_ref[0] = product(inc_ref[...] - near, inv_ref[...])
        out_ref[1] = product(twin_inc_ref[...] - twin_near, twin_inv_ref[...])

    vmem = pl.BlockSpec(memory_space=pltpu.VMEM)
    return pl.pallas_call(
        body,
        out_shape=jax.ShapeDtypeStruct((2, waves, size), F32),
        in_specs=[pl.BlockSpec(memory_space=pltpu.SMEM)] + [vmem] * 5,
        out_specs=vmem,
        name="first_density",
    )(plane, partials, incident, twin_incident, inverse, twin_inverse)


def last_density(ids, core, mine, partner, kernel, driven, inverse):
    near, size, _ = kernel.shape
    waves = driven.shape[0]

    def body(ids_ref, core_ref, mine_ref, partner_ref, kernel_ref, driven_ref, inv_ref, out_ref):
        total = jnp.zeros((waves, size), F32)
        for slot in range(near):
            source = ids_ref[slot]
            chip = (source // 2) % 16
            plane = source // 32
            same = (source % 2) == core_ref[0]
            block = jnp.where(same, mine_ref[chip, plane], partner_ref[chip, plane])
            total = total + product(block, kernel_ref[slot])
        out_ref[...] = product(driven_ref[...] - total, inv_ref[...])

    vmem = pl.BlockSpec(memory_space=pltpu.VMEM)
    smem = pl.BlockSpec(memory_space=pltpu.SMEM)
    return pl.pallas_call(
        body,
        out_shape=jax.ShapeDtypeStruct((waves, size), F32),
        in_specs=[smem, smem] + [vmem] * 5,
        out_specs=vmem,
        name="last_density",
    )(ids, core, mine, partner, kernel, driven, inverse)


def shards(history, incident, kernel, near_blocks, self_inverse):
    lag_dev, waves, size = history.shape
    kernel_rows = kernel[0]
    inverse = self_inverse[0]
    near = near_blocks.shape[2]
    planes = lax.axis_size("z_hi")
    peers = lax.axis_size(PLANE)
    groups = lax.axis_size("lags")
    plane = lax.axis_index("z_hi")
    core = lax.axis_index("core")
    swap = [(0, 1), (1, 0)]

    before = lax.ppermute(history[lag_dev - 1], "lags", [(g, g + 1) for g in range(groups - 1)])
    window = jnp.concatenate([before[None], history], axis=0)
    twin_window = lax.ppermute(window, "z_hi", swap)
    twin_inverse = lax.ppermute(inverse, "z_hi", swap)
    twin_incident = lax.ppermute(incident[0], "z_hi", swap)

    ids = jnp.bitwise_xor(near_blocks[0], plane * peers)
    hit = ids.reshape(lag_dev * near, 1) == jnp.arange(planes * peers, dtype=jnp.int32)[None, :]
    lag_of = jnp.repeat(jnp.arange(lag_dev, dtype=jnp.int32), near)[:, None]
    wanted = jnp.sum(jnp.where(hit, lag_of, 0), axis=0)
    wanted = jnp.pad(wanted.reshape(planes, peers).T[:, None, :], ((0, 0), (0, 0), (0, 128 - planes)))
    table = lax.all_to_all(wanted, PLANE, 0, 0, tiled=True)[:, 0, :planes]

    received0 = lax.all_to_all(pack(table, window, twin_window, 1), PLANE, 0, 0, tiled=True)
    received1 = lax.all_to_all(pack(table, window, twin_window, 0), PLANE, 0, 0, tiled=True)

    partial0 = near_partial(ids, received0, kernel_rows, "near0")
    spread = jnp.broadcast_to(partial0[None], (planes * groups, waves, size))
    partials = lax.all_to_all(spread, ("z_hi", "lags"), 0, 0, tiled=True)
    density0 = first_density(plane[None], partials, incident[0], twin_incident, inverse, twin_inverse)

    chips = peers // 2
    spread = jnp.broadcast_to(density0[None], (chips, planes, waves, size))
    mine = lax.all_to_all(spread, ("y", "x"), 0, 0, tiled=True)
    partner = lax.ppermute(mine, "core", swap)

    partial1 = near_partial(ids, received1, kernel_rows, "near1")
    driven = incident[1] - partial1
    for group in range(1, groups):
        driven = driven - lax.ppermute(partial1, "lags", [(group, 0)])

    density1 = last_density(ids[0], core[None], mine, partner, kernel_rows[0], driven, inverse)
    result = jnp.where(lax.axis_index("lags") == 0, density1, 0.0)
    for group in range(1, groups):
        result = result + lax.ppermute(density1, "lags", [(0, group)])
    return jnp.stack([density0[0], result])


def solution(mesh):
    shape = (2, 4, 4, 2, mesh.shape["lags"])
    parts = Mesh(mesh.devices.reshape(shape), ROWS + ("lags",))
    in_specs = (
        P("lags", None, ROWS),
        P(None, None, ROWS),
        P(ROWS, "lags", None, None, None),
        P(ROWS, "lags", None),
        P(ROWS, None, None),
    )
    out_specs = P(None, None, ROWS)
    return jax.shard_map(shards, mesh=parts, in_specs=in_specs, out_specs=out_specs, check_vma=False)
```

time: 292 us -> 152 us (0.52)
  waiting for transfers between devices: 196 us -> 48.3 us
  starting transfers between devices: 1.41 us -> 44.6 us
  Pallas kernels: 0 us -> 26.7 us
  matrix products: 19.5 us -> 0 us
  blocking collectives: 31.8 us -> 13.5 us
  between operations: 13.5 us -> 0.19 us
  local copies, waits for them, and re-layouts: 25.5 us -> 12.5 us
    all_gather x2 -> x0, waiting for transfers between devices: 176 us -> none  [the longest x1 126 us: shards(): gathered = lax.all_gather(history, 'rows', axis=2, tiled=True)]
    all_to_all x0 -> x4, waiting for transfers between devices: none -> 36.4 us  [the longest x1 14.9 us: shards(): lax.all_to_all(pack(table, window, twin_window, 1), PLANE, 0, 0, tiled=True)]
    psum x2 -> x0, blocking collectives: 31.8 us -> none  [solve_from(): near_field = lax.psum(partial_value, 'lags')]
    pallas_call x0 -> x6, Pallas kernels: none -> 26.7 us  [the longest x2 17.8 us: near_partial(): pl.pallas_call(body, grid=(lag_dev,), out_shape=jax.ShapeDtypeStruct((wav...]
    ppermute x1 -> x11, starting transfers between devices: 1.36 us -> 25.1 us  [the longest x1 6.38 us: shards(): twin_window = lax.ppermute(window, 'z_hi', swap)]
    all_to_all x0 -> x4, starting transfers between devices: none -> 19.5 us  [the longest x1 5.18 us: shards(): lax.all_to_all(pack(table, window, twin_window, 1), PLANE, 0, 0, tiled=True)]
    dot_general x4 -> x0, matrix products: 19.5 us -> none  [the longest x2 18.4 us: solve_from(): jnp.einsum('jkwc,jkcr->wr', picked, kernel_rows, precision=highest)]
    reshape x2 -> x1, local copies, waits for them, and re-layouts: 15.5 us -> 0.08 us  [shards(): wanted.reshape(planes, peers).T[:, None, :]]
  transfers between devices with their start and end apart: 3 -> 15, of which waited for: 3 -> 10; matrix products, arithmetic and copies ran while one was open for 1% -> 5% of each run, Pallas kernels for 0% -> 13%
where the time goes in v1:
time: 152 us; the launch traced here: 150 us
  waiting for transfers between devices  48.3 us (32%)
  starting transfers between devices  44.6 us (29%)
  Pallas kernels  26.7 us (18%)
  blocking collectives  13.5 us (9%)
  local copies, waits for them, and re-layouts  12.5 us (8%)
  other arithmetic  4.27 us (3%)
    pallas_call x2, Pallas kernels, near_partial(): pl.pallas_call(body, grid=(lag_dev,), out_shape=jax.ShapeDtypeStruct((wav...  17.8 us
    all_to_all x1, waiting for transfers between devices, shards(): lax.all_to_all(pack(table, window, twin_window, 1), PLANE, 0, 0, tiled=True)  14.9 us
    all_to_all x1, blocking collectives, shards(): table = lax.all_to_all(wanted, PLANE, 0, 0, tiled=True)[:, 0, :planes]  13.5 us
    all_to_all x1, waiting for transfers between devices, shards(): lax.all_to_all(pack(table, window, twin_window, 0), PLANE, 0, 0, tiled=True)  13.1 us
    all_to_all x1, waiting for transfers between devices, shards(): mine = lax.all_to_all(spread, ('y', 'x'), 0, 0, tiled=True)  8.39 us
    ppermute x1, starting transfers between devices, shards(): twin_window = lax.ppermute(window, 'z_hi', swap)  6.38 us
    ppermute x1, starting transfers between devices, shards(): twin_incident = lax.ppermute(incident[0], 'z_hi', swap)  6.01 us
    ppermute x3, waiting for transfers between devices, shards(): driven = driven - lax.ppermute(partial1, 'lags', [(group, 0)])  5.75 us
  transfers between devices with their start and end apart: 15, of which 10 were waited for; matrix products, arithmetic and copies ran while one was open for 5% of the time, Pallas kernels for 13%

profile of v1, /device:TPU:2, one launch (start us, length us, event | category | flops | bytes accessed | tf_op | source)
XLA Modules:
  0.0 150.0 jit_solution(5526194852143169840)
XLA Ops:
  0.7 3.8 %collective-permute-start = (f32[16,256]{1,0:T(8,128)S(1)}, f32[16,256]{1,0:T(8,128)S(1)}, u32[]{:S(2)}, u32[]{:S(2)}) collective-permute-start(f32[16,256]{1,0:T(8,128)S(1)} %slice_bitcast_fusion.2), channel_id=1, source_target_pairs={{0,1},{1,2},{2,3},{4,5},{5,6},{6,7},{8,9},{9,10},{10,11},{12,13},{... | collective-permute-start | bytes 49160 | tf_op jit(solution)/shard_map/ppermute | solution.py:147
  6.9 6.4 %collective-permute-start.1 = (f32[9,16,256]{2,1,0:T(8,128)S(1)}, f32[9,16,256]{2,1,0:T(8,128)S(1)}, u32[]{:S(2)}, u32[]{:S(2)}) collective-permute-start(f32[9,16,256]{2,1,0:T(8,128)S(1)} %pad_maximum_fusion.own_ref), channel_id=1, source_target_pairs={{0,128},{128,0},{1,129},{129,1},{2,130},{130,2},{3,131},{131,3},{4... | collective-permute-start | bytes 442376 | tf_op jit(solution)/shard_map/ppermute | solution.py:149
  13.7 13.5 %all_to_all.25 = s32[32,1,128]{2,1,0:T(1,128)} all-to-all(s32[32,1,128]{2,1,0:T(1,128)S(1)} %pad.4.clone), channel_id=1, replica_groups=mesh['z_hi'=2,'y'=4,'x'=4,'core'=2,'lags'=4] {'y','x','core'}, dimensions={0} | all-to-all | bytes 32768 | tf_op jit(solution)/shard_map/all_to_all | solution.py:158
  28.0 2.1 %pack1.1 = f32[32,2,16,256]{3,2,1,0:T(8,128)} custom-call(s32[32,2]{1,0:T(8,128)} %bitcast.35, f32[9,16,256]{2,1,0:T(8,128)} %copy-done.3, f32[9,16,256]{2,1,0:T(8,128)} %copy-done.4), custom_call_target="tpu_custom_call" | custom-call | tf_op jit(solution)/shard_map/pack1/pallas_call | solution.py:41
  30.0 5.2 %all-to-all-start.1 = ((f32[32,2,16,256]{3,2,1,0:T(8,128)}), f32[32,2,16,256]{3,2,1,0:T(8,128)S(1)}, u32[]{:S(2)}, u32[]{:S(2)}) async-start(f32[32,2,16,256]{3,2,1,0:T(8,128)} %pack1.1), calls=%async_computation.1 | async-start | bytes 2097152 | tf_op jit(solution)/shard_map/all_to_all | solution.py:160
  36.4 14.9 %all-to-all-done.1.received_ref = f32[32,2,16,256]{3,2,1,0:T(8,128)S(1)} async-done(((f32[32,2,16,256]{3,2,1,0:T(8,128)}), f32[32,2,16,256]{3,2,1,0:T(8,128)S(1)}, u32[]{:S(2)}, u32[]{:S(2)}) %all-to-all-start.1) | async-done | bytes 1048608 | tf_op jit(solution)/shard_map/all_to_all | solution.py:160
  52.3 8.9 %near0.1 = f32[16,256]{1,0:T(8,128)} custom-call(s32[8,6]{1,0:T(8,128)} %fusion.3.ids_ref, f32[32,2,16,256]{3,2,1,0:T(8,128)} %copy-done, f32[8,6,256,256]{3,2,1,0:T(8,128)} %bitcast.30), custom_call_target="tpu_custom_call" | custom-call | tf_op jit(solution)/shard_map/near0/pallas_call | solution.py:70
  61.2 1.4 broadcast_in_dim.53
  62.5 4.5 %all-to-all-start.2 = ((f32[8,16,256]{2,1,0:T(8,128)}), f32[8,16,256]{2,1,0:T(8,128)S(1)}, u32[]{:S(2)}, u32[]{:S(2)}) async-start(f32[8,16,256]{2,1,0:T(8,128)} %broadcast_in_dim.53), calls=%async_computation.2 | async-start | bytes 262144 | tf_op jit(solution)/shard_map/all_to_all | solution.py:165
  67.0 6.0 %collective-permute-start.2 = (f32[16,256]{1,0:T(8,128)S(1)}, f32[16,256]{1,0:T(8,128)S(1)}, u32[]{:S(2)}, u32[]{:S(2)}) collective-permute-start(f32[16,256]{1,0:T(8,128)S(1)} %slice_bitcast_fusion.1.inc_ref), channel_id=1, source_target_pairs={{0,128},{128,0},{1,129},{129,1},{2,130},{130,2},{3,131},{131,3},{4... | collective-permute-start | bytes 49160 | tf_op jit(solution)/shard_map/ppermute | solution.py:151
  73.1 3.8 %collective-permute-done.2.twin_inc_ref = f32[16,256]{1,0:T(8,128)S(1)} collective-permute-done((f32[16,256]{1,0:T(8,128)S(1)}, f32[16,256]{1,0:T(8,128)S(1)}, u32[]{:S(2)}, u32[]{:S(2)}) %collective-permute-start.2) | collective-permute-done | bytes 16416 | tf_op jit(solution)/shard_map/ppermute | solution.py:151
  77.6 1.9 %first_density.1 = f32[2,16,256]{2,1,0:T(8,128)} custom-call(s32[1]{0:T(128)} %bitcast.plane_ref, f32[8,16,256]{2,1,0:T(8,128)} %copy-done.5, f32[16,256]{1,0:T(8,128)} %copy-done.8, f32[16,256]{1,0:T(8,128)} %copy-done.10, f32[256,256]{1,0:T(8,128)} %bitcast.33, f32[256,256]{1,0:T(8,128)} %copy-done.7), custom_call_target="tpu_custom_call" | custom-call | tf_op jit(solution)/shard_map/first_density/pallas_call | solution.py:100
  79.6 1.7 %broadcast_in_dim.55 = f32[16,2,16,256]{3,2,1,0:T(8,128)} broadcast(f32[2,16,256]{2,1,0:T(8,128)} %first_density.1), dimensions={1,2,3} | broadcast | bytes 557056 | tf_op jit(solution)/shard_map/broadcast_in_dim | solution.py:169
  81.3 4.8 %all-to-all-start.3 = ((f32[16,2,16,256]{3,2,1,0:T(8,128)}), f32[16,2,16,256]{3,2,1,0:T(8,128)S(1)}, u32[]{:S(2)}, u32[]{:S(2)}) async-start(f32[16,2,16,256]{3,2,1,0:T(8,128)} %broadcast_in_dim.55), calls=%async_computation.3 | async-start | bytes 1048576 | tf_op jit(solution)/shard_map/all_to_all | solution.py:170
  86.1 2.1 %pack0.1 = f32[32,2,16,256]{3,2,1,0:T(8,128)} custom-call(s32[32,2]{1,0:T(8,128)} %bitcast.36, f32[9,16,256]{2,1,0:T(8,128)} %copy-done.3, f32[9,16,256]{2,1,0:T(8,128)} %copy-done.4), custom_call_target="tpu_custom_call" | custom-call | tf_op jit(solution)/shard_map/pack0/pallas_call | solution.py:41
  88.1 8.4 %all-to-all-done.3.mine_ref = f32[16,2,16,256]{3,2,1,0:T(8,128)S(1)} async-done(((f32[16,2,16,256]{3,2,1,0:T(8,128)}), f32[16,2,16,256]{3,2,1,0:T(8,128)S(1)}, u32[]{:S(2)}, u32[]{:S(2)}) %all-to-all-start.3) | async-done | bytes 524320 | tf_op jit(solution)/shard_map/all_to_all | solution.py:170
  96.5 5.0 %all-to-all-start.4 = ((f32[32,2,16,256]{3,2,1,0:T(8,128)}), f32[32,2,16,256]{3,2,1,0:T(8,128)S(1)}, u32[]{:S(2)}, u32[]{:S(2)}) async-start(f32[32,2,16,256]{3,2,1,0:T(8,128)} %pack0.1), calls=%async_computation.4 | async-start | bytes 2097152 | tf_op jit(solution)/shard_map/all_to_all | solution.py:161
  101.8 2.8 %slice_bitcast_fusion.kernel_ref = f32[6,256,256]{2,1,0:T(8,128)} fusion(f32[1,8,6,256,256]{4,3,2,1,0:T(8,128)} %param.7), kind=kLoop, calls=%fused_computation | loop fusion | bytes 3145728 | tf_op jit(solution)/shard_map/squeeze | solution.py:178
  104.6 13.1 %all-to-all-done.4.received_ref = f32[32,2,16,256]{3,2,1,0:T(8,128)S(1)} async-done(((f32[32,2,16,256]{3,2,1,0:T(8,128)}), f32[32,2,16,256]{3,2,1,0:T(8,128)S(1)}, u32[]{:S(2)}, u32[]{:S(2)}) %all-to-all-start.4) | async-done | bytes 1048608 | tf_op jit(solution)/shard_map/all_to_all | solution.py:161
  118.7 8.9 %near1.1 = f32[16,256]{1,0:T(8,128)} custom-call(s32[8,6]{1,0:T(8,128)} %fusion.3.ids_ref, f32[32,2,16,256]{3,2,1,0:T(8,128)} %copy-done.1, f32[8,6,256,256]{3,2,1,0:T(8,128)} %bitcast.31), custom_call_target="tpu_custom_call" | custom-call | tf_op jit(solution)/shard_map/near1/pallas_call | solution.py:70
  127.5 1.3 collective-permute-start.5
  128.8 1.3 collective-permute-start.6
  130.1 1.3 collective-permute-start.7
  132.0 1.4 collective-permute-done.5
  133.4 2.2 %collective-permute-done.6 = f32[16,256]{1,0:T(8,128)S(1)} collective-permute-done((f32[16,256]{1,0:T(8,128)}, f32[16,256]{1,0:T(8,128)S(1)}, u32[]{:S(2)}, u32[]{:S(2)}) %collective-permute-start.6) | collective-permute-done | bytes 16416 | tf_op jit(solution)/shard_map/ppermute | solution.py:176
  135.6 2.2 %collective-permute-done.7 = f32[16,256]{1,0:T(8,128)S(1)} collective-permute-done((f32[16,256]{1,0:T(8,128)}, f32[16,256]{1,0:T(8,128)S(1)}, u32[]{:S(2)}, u32[]{:S(2)}) %collective-permute-start.7) | collective-permute-done | bytes 16416 | tf_op jit(solution)/shard_map/ppermute | solution.py:176
  137.8 1.3 fusion.2.driven_ref
  139.9 2.9 %last_density.1 = f32[16,256]{1,0:T(8,128)} custom-call(s32[6]{0:T(128)} %slice_bitcast_fusion.3.ids_ref, s32[1]{0:T(128)} %bitcast.11.core_ref, f32[16,2,16,256]{3,2,1,0:T(8,128)} %copy-done.2, f32[16,2,16,256]{3,2,1,0:T(8,128)} %copy-done.6, f32[6,256,256]{2,1,0:T(8,128)} %slice_bitcast_fusion.kernel_ref, f32[16,256]{1,0:T(8,128)} %fusion.2.driven_ref, ...), custom_call_target="tpu_custom_call" | custom-call | tf_op jit(solution)/shard_map/last_density/pallas_call | solution.py:126
  142.8 1.6 %collective-permute-start.10 = (f32[16,256]{1,0:T(8,128)}, f32[16,256]{1,0:T(8,128)S(1)}, u32[]{:S(2)}, u32[]{:S(2)}) collective-permute-start(f32[16,256]{1,0:T(8,128)} %last_density.1), channel_id=1, source_target_pairs={{0,3},{4,7},{8,11},{12,15},{16,19},{20,23},{24,27},{28,31},{32,35}... | collective-permute-start | bytes 49160 | tf_op jit(solution)/shard_map/ppermute | solution.py:181
  144.4 1.3 collective-permute-start.8
  145.7 1.3 collective-permute-start.9
  147.4 1.3 collective-permute-done.9
  (49 shorter events, 11.3 us)
Async XLA Ops:
  0.0 67.0 %copy-start.9 = (f32[2,16,256]{2,1,0:T(8,128)S(1)}, f32[2,16,256]{2,1,0:T(8,128)}, u32[]{:S(2)}) copy-start(f32[2,16,256]{2,1,0:T(8,128)} %param.6) | copy-start | bytes 98308
  0.7 5.2 %collective-permute-start = (f32[16,256]{1,0:T(8,128)S(1)}, f32[16,256]{1,0:T(8,128)S(1)}, u32[]{:S(2)}, u32[]{:S(2)}) collective-permute-start(f32[16,256]{1,0:T(8,128)S(1)} %slice_bitcast_fusion.2), channel_id=1, source_target_pairs={{0,1},{1,2},{2,3},{4,5},{5,6},{6,7},{8,9},{9,10},{10,11},{12,13},{... | collective-permute-start | bytes 49160 | tf_op jit(solution)/shard_map/ppermute | solution.py:147
  6.9 20.4 %copy-start.3 = (f32[9,16,256]{2,1,0:T(8,128)}, f32[9,16,256]{2,1,0:T(8,128)S(1)}, u32[]{:S(2)}) copy-start(f32[9,16,256]{2,1,0:T(8,128)S(1)} %pad_maximum_fusion.own_ref) | copy-start | bytes 442372
  6.9 20.4 %collective-permute-start.1 = (f32[9,16,256]{2,1,0:T(8,128)S(1)}, f32[9,16,256]{2,1,0:T(8,128)S(1)}, u32[]{:S(2)}, u32[]{:S(2)}) collective-permute-start(f32[9,16,256]{2,1,0:T(8,128)S(1)} %pad_maximum_fusion.own_ref), channel_id=1, source_target_pairs={{0,128},{128,0},{1,129},{129,1},{2,130},{130,2},{3,131},{131,3},{4... | collective-permute-start | bytes 442376 | tf_op jit(solution)/shard_map/ppermute | solution.py:149
  27.3 0.7 copy-start.4
  30.0 21.3 %all-to-all-start.1 = ((f32[32,2,16,256]{3,2,1,0:T(8,128)}), f32[32,2,16,256]{3,2,1,0:T(8,128)S(1)}, u32[]{:S(2)}, u32[]{:S(2)}) async-start(f32[32,2,16,256]{3,2,1,0:T(8,128)} %pack1.1), calls=%async_computation.1 | async-start | bytes 2097152 | tf_op jit(solution)/shard_map/all_to_all | solution.py:160
  35.2 41.7 %collective-permute-start.3 = (f32[256,256]{1,0:T(8,128)}, f32[256,256]{1,0:T(8,128)S(1)}, u32[]{:S(2)}, u32[]{:S(2)}) collective-permute-start(f32[256,256]{1,0:T(8,128)} %bitcast.32), channel_id=1, source_target_pairs={{0,128},{128,0},{1,129},{129,1},{2,130},{130,2},{3,131},{131,3},{4... | collective-permute-start | bytes 786440 | tf_op jit(solution)/shard_map/ppermute | solution.py:150
  51.3 1.0 copy-start
  62.5 14.4 %all-to-all-start.2 = ((f32[8,16,256]{2,1,0:T(8,128)}), f32[8,16,256]{2,1,0:T(8,128)S(1)}, u32[]{:S(2)}, u32[]{:S(2)}) async-start(f32[8,16,256]{2,1,0:T(8,128)} %broadcast_in_dim.53), calls=%async_computation.2 | async-start | bytes 262144 | tf_op jit(solution)/shard_map/all_to_all | solution.py:165
  67.0 9.9 %copy-start.8 = (f32[16,256]{1,0:T(8,128)}, f32[16,256]{1,0:T(8,128)S(1)}, u32[]{:S(2)}) copy-start(f32[16,256]{1,0:T(8,128)S(1)} %slice_bitcast_fusion.1.inc_ref) | copy-start | bytes 49156
  67.0 9.8 %collective-permute-start.2 = (f32[16,256]{1,0:T(8,128)S(1)}, f32[16,256]{1,0:T(8,128)S(1)}, u32[]{:S(2)}, u32[]{:S(2)}) collective-permute-start(f32[16,256]{1,0:T(8,128)S(1)} %slice_bitcast_fusion.1.inc_ref), channel_id=1, source_target_pairs={{0,128},{128,0},{1,129},{129,1},{2,130},{130,2},{3,131},{131,3},{4... | collective-permute-start | bytes 49160 | tf_op jit(solution)/shard_map/ppermute | solution.py:151
  76.9 0.6 copy-start.10
  76.9 0.7 copy-start.7
  76.9 0.7 copy-start.5
  79.6 69.8 %slice-start = ((f32[2,16,256]{2,1,0:T(8,128)}), f32[1,16,256]{2,1,0:T(8,128)S(1)}, s32[]{:S(2)}) async-start(f32[2,16,256]{2,1,0:T(8,128)} %first_density.1), calls=%async_computation.5 | async-start | bytes 32768 | tf_op jit(solution)/shard_map/slice | solution.py:182
  81.3 15.2 %all-to-all-start.3 = ((f32[16,2,16,256]{3,2,1,0:T(8,128)}), f32[16,2,16,256]{3,2,1,0:T(8,128)S(1)}, u32[]{:S(2)}, u32[]{:S(2)}) async-start(f32[16,2,16,256]{3,2,1,0:T(8,128)} %broadcast_in_dim.55), calls=%async_computation.3 | async-start | bytes 1048576 | tf_op jit(solution)/shard_map/all_to_all | solution.py:170
  96.5 42.6 %copy-start.2 = (f32[16,2,16,256]{3,2,1,0:T(8,128)}, f32[16,2,16,256]{3,2,1,0:T(8,128)S(1)}, u32[]{:S(2)}) copy-start(f32[16,2,16,256]{3,2,1,0:T(8,128)S(1)} %all-to-all-done.3.mine_ref) | copy-start | bytes 1572868
  96.5 21.2 %all-to-all-start.4 = ((f32[32,2,16,256]{3,2,1,0:T(8,128)}), f32[32,2,16,256]{3,2,1,0:T(8,128)S(1)}, u32[]{:S(2)}, u32[]{:S(2)}) async-start(f32[32,2,16,256]{3,2,1,0:T(8,128)} %pack0.1), calls=%async_computation.4 | async-start | bytes 2097152 | tf_op jit(solution)/shard_map/all_to_all | solution.py:161
  101.6 37.5 %collective-permute-start.4 = (f32[16,2,16,256]{3,2,1,0:T(8,128)S(1)}, f32[16,2,16,256]{3,2,1,0:T(8,128)S(1)}, u32[]{:S(2)}, u32[]{:S(2)}) collective-permute-start(f32[16,2,16,256]{3,2,1,0:T(8,128)S(1)} %all-to-all-done.3.mine_ref), channel_id=1, source_target_pairs={{0,4},{4,0},{1,5},{5,1},{2,6},{6,2},{3,7},{7,3},{8,12},{12,8},{9,1... | collective-permute-start | bytes 1572872 | tf_op jit(solution)/shard_map/ppermute | solution.py:171
  117.7 1.0 copy-start.1
  127.5 5.8 %collective-permute-start.5 = (f32[16,256]{1,0:T(8,128)}, f32[16,256]{1,0:T(8,128)S(1)}, u32[]{:S(2)}, u32[]{:S(2)}) collective-permute-start(f32[16,256]{1,0:T(8,128)} %near1.1), channel_id=1, source_target_pairs={{1,0},{5,4},{9,8},{13,12},{17,16},{21,20},{25,24},{29,28},{33,32},... | collective-permute-start | bytes 49160 | tf_op jit(solution)/shard_map/ppermute | solution.py:176
  128.8 6.7 %collective-permute-start.6 = (f32[16,256]{1,0:T(8,128)}, f32[16,256]{1,0:T(8,128)S(1)}, u32[]{:S(2)}, u32[]{:S(2)}) collective-permute-start(f32[16,256]{1,0:T(8,128)} %near1.1), channel_id=1, source_target_pairs={{2,0},{6,4},{10,8},{14,12},{18,16},{22,20},{26,24},{30,28},{34,32}... | collective-permute-start | bytes 49160 | tf_op jit(solution)/shard_map/ppermute | solution.py:176
  130.1 7.6 %collective-permute-start.7 = (f32[16,256]{1,0:T(8,128)}, f32[16,256]{1,0:T(8,128)S(1)}, u32[]{:S(2)}, u32[]{:S(2)}) collective-permute-start(f32[16,256]{1,0:T(8,128)} %near1.1), channel_id=1, source_target_pairs={{3,0},{7,4},{11,8},{15,12},{19,16},{23,20},{27,24},{31,28},{35,32}... | collective-permute-start | bytes 49160 | tf_op jit(solution)/shard_map/ppermute | solution.py:176
  139.1 0.8 copy-start.6
  142.8 4.2 %collective-permute-start.10 = (f32[16,256]{1,0:T(8,128)}, f32[16,256]{1,0:T(8,128)S(1)}, u32[]{:S(2)}, u32[]{:S(2)}) collective-permute-start(f32[16,256]{1,0:T(8,128)} %last_density.1), channel_id=1, source_target_pairs={{0,3},{4,7},{8,11},{12,15},{16,19},{20,23},{24,27},{28,31},{32,35}... | collective-permute-start | bytes 49160 | tf_op jit(solution)/shard_map/ppermute | solution.py:181
  144.4 2.9 %collective-permute-start.8 = (f32[16,256]{1,0:T(8,128)}, f32[16,256]{1,0:T(8,128)S(1)}, u32[]{:S(2)}, u32[]{:S(2)}) collective-permute-start(f32[16,256]{1,0:T(8,128)} %last_density.1), channel_id=1, source_target_pairs={{0,1},{4,5},{8,9},{12,13},{16,17},{20,21},{24,25},{28,29},{32,33},... | collective-permute-start | bytes 49160 | tf_op jit(solution)/shard_map/ppermute | solution.py:181
  145.7 2.9 %collective-permute-start.9 = (f32[16,256]{1,0:T(8,128)}, f32[16,256]{1,0:T(8,128)S(1)}, u32[]{:S(2)}, u32[]{:S(2)}) collective-permute-start(f32[16,256]{1,0:T(8,128)} %last_density.1), channel_id=1, source_target_pairs={{0,2},{4,6},{8,10},{12,14},{16,18},{20,22},{24,26},{28,30},{32,34}... | collective-permute-start | bytes 49160 | tf_op jit(solution)/shard_map/ppermute | solution.py:181

commit v2 on v1

v2 whole, which is shorter than its diff:
```python
import jax
import jax.numpy as jnp
from jax import lax
from jax.experimental import pallas as pl
from jax.experimental.pallas import tpu as pltpu
from jax.sharding import Mesh
from jax.sharding import PartitionSpec as P


PLANE = ("y", "x", "core")
ROWS = ("z_hi",) + PLANE
F32 = jnp.float32
BF16 = jnp.bfloat16
VMEM = pl.BlockSpec(memory_space=pltpu.VMEM)
SMEM = pl.BlockSpec(memory_space=pltpu.SMEM)
PARAMS = pltpu.CompilerParams(vmem_limit_bytes=8 << 20)


def resident(array):
    return pltpu.with_memory_space_constraint(array, pltpu.VMEM)


def call(body, out, in_specs, operands, aliases=None):
    held = [resident(a) if s is VMEM else a for a, s in zip(operands, in_specs)]
    return pl.pallas_call(
        body,
        out_shape=out,
        in_specs=in_specs,
        out_specs=jax.tree.map(lambda _: VMEM, out),
        input_output_aliases=aliases or {},
        compiler_params=PARAMS,
    )(*held)


def split(value):
    high = value.astype(BF16)
    low = (value - high.astype(F32)).astype(BF16)
    return high, low


def product(left, right_high, right_low):
    waves = left.shape[0]
    left_high, left_low = split(left)
    both = jnp.concatenate([left_high, left_low], axis=0)
    first = jnp.dot(both, right_high, preferred_element_type=F32)
    second = jnp.dot(left_high, right_low, preferred_element_type=F32)
    return first[:waves] + (first[waves:] + second)


def lag_table(near_t, base, peers, lanes):
    near, _, lag_dev = near_t.shape

    def body(near_ref, base_ref, out_ref):
        ids = lax.broadcasted_iota(jnp.int32, (peers, lanes), 1) * peers
        ids = ids + lax.broadcasted_iota(jnp.int32, (peers, lanes), 0)
        table = jnp.zeros((peers, lanes), jnp.int32)
        for slot in range(near):
            for lag in range(1, lag_dev):
                source = jnp.bitwise_xor(near_ref[slot, 0, lag], base_ref[0])
                table = jnp.where(ids == source, lag, table)
        out_ref[...] = table

    return call(body, jax.ShapeDtypeStruct((peers, lanes), jnp.int32), [SMEM, SMEM], [near_t, base])


def pack(table, own, twin, before, twin_before):
    peers, _, _ = table.shape
    block = own.shape[1:]
    out = pltpu.VMEM((peers, 2, 2) + block, F32)

    def body(table_ref, own_ref, twin_ref, before_ref, twin_before_ref, out_ref):
        edges = (before_ref[...], twin_before_ref[...])
        for peer in range(peers):
            for plane, ref in enumerate((own_ref, twin_ref)):
                lag = table_ref[peer, 0, plane]
                out_ref[peer, 0, plane] = ref[lag]
                nearer = ref[jnp.maximum(lag - 1, 0)]
                out_ref[peer, 1, plane] = jnp.where(lag == 0, edges[plane], nearer)

    return call(body, out, [SMEM] + [VMEM] * 4, [table, own, twin, before, twin_before])


def split_kernel(kernel):
    lag_dev, near, size, _ = kernel.shape

    def body(kernel_ref, high_ref, low_ref, first_high_ref, first_low_ref):
        lag = pl.program_id(0)
        high, low = split(kernel_ref[0])
        high_ref[lag] = high
        low_ref[lag] = low

        @pl.when(lag == 0)
        def _():
            first_high_ref[...] = high
            first_low_ref[...] = low

    out = pltpu.VMEM(kernel.shape, BF16)
    first = pltpu.VMEM(kernel.shape[1:], BF16)
    return pl.pallas_call(
        body,
        grid=(lag_dev,),
        out_shape=(out, out, first, first),
        in_specs=[pl.BlockSpec((1, near, size, size), lambda lag: (lag, 0, 0, 0))],
        out_specs=(VMEM,) * 4,
        compiler_params=PARAMS,
        name="split_kernel",
    )(kernel)


def near_partial(near_t, base, received, high, low, copies):
    lag_dev, near, size, _ = high.shape
    peers, steps, _, waves, _ = received.shape

    def body(near_ref, base_ref, received_ref, high_ref, low_ref, out_ref, rest_ref):
        total = jnp.zeros((steps * waves, size), F32)
        for lag in range(lag_dev):
            for slot in range(near):
                source = jnp.bitwise_xor(near_ref[slot, 0, lag], base_ref[0])
                peer, plane = source % peers, source // peers
                block = jnp.concatenate([received_ref[peer, step, plane] for step in range(steps)], axis=0)
                total = total + product(block, high_ref[lag, slot], low_ref[lag, slot])
        for copy in range(copies):
            out_ref[copy] = total[:waves]
        rest_ref[...] = total[waves:]

    out = (pltpu.VMEM((copies, waves, size), F32), pltpu.VMEM((waves, size), F32))
    return call(body, out, [SMEM, SMEM] + [VMEM] * 3, [near_t, base, received, high, low])


def first_density(base, partials, incident, twin_incident, inverse, twin_inverse, chips, peers):
    groups = partials.shape[0] // 2
    waves, size = twin_incident.shape

    def body(base_ref, partials_ref, inc_ref, twin_inc_ref, inv_ref, twin_inv_ref, out_ref):
        own = (base_ref[0] // peers) * groups
        twin = groups - own
        near = partials_ref[own]
        twin_near = partials_ref[twin]
        for group in range(1, groups):
            near = near + partials_ref[own + group]
            twin_near = twin_near + partials_ref[twin + group]
        density = product(inc_ref[0] - near, *split(inv_ref[...]))
        twin_density = product(twin_inc_ref[...] - twin_near, *split(twin_inv_ref[...]))
        for chip in range(chips):
            out_ref[chip, 0] = density
            out_ref[chip, 1] = twin_density

    out = pltpu.VMEM((chips, 2, waves, size), F32)
    operands = [base, partials, incident, twin_incident, inverse, twin_inverse]
    return call(body, out, [SMEM] + [VMEM] * 5, operands)


def last_density(near_t, base, core, mine, partner, high, low, driven, inverse):
    near = near_t.shape[0]
    waves, size = driven.shape
    chips = mine.shape[0]

    def body(near_ref, base_ref, core_ref, mine_ref, partner_ref, high_ref, low_ref, driven_ref, inv_ref, out_ref):
        total = jnp.zeros((waves, size), F32)
        for slot in range(near):
            source = jnp.bitwise_xor(near_ref[slot, 0, 0], base_ref[0])
            chip = (source // 2) % chips
            plane = source // (2 * chips)
            same = (source % 2) == core_ref[0]
            block = jnp.where(same, mine_ref[chip, plane], partner_ref[chip, plane])
            total = total + product(block, high_ref[slot], low_ref[slot])
        out_ref[...] = product(driven_ref[...] - total, *split(inv_ref[...]))

    out = pltpu.VMEM((waves, size), F32)
    operands = [near_t, base, core, mine, partner, high, low, driven, inverse]
    return call(body, out, [SMEM] * 3 + [VMEM] * 6, operands)


def shards(history, incident, kernel, near_blocks, self_inverse):
    lag_dev, _, size = history.shape
    inverse = self_inverse[0]
    planes = lax.axis_size("z_hi")
    peers = lax.axis_size(PLANE)
    chips = peers // 2
    groups = lax.axis_size("lags")
    plane = lax.axis_index("z_hi")
    core = lax.axis_index("core")[None]
    base = (plane * peers)[None]
    near_t = jnp.transpose(near_blocks, (2, 0, 1))
    swap = [(0, 1), (1, 0)]

    def exchange(array, axes):
        return lax.all_to_all(array, axes, 0, 0, tiled=True)

    table = lag_table(near_t, base, peers, 128)
    table = exchange(table[:, None, :], PLANE)
    twin = lax.ppermute(history, "z_hi", swap)

    edge = history[lag_dev - 1]
    before = lax.ppermute(edge, "lags", [(g, g + 1) for g in range(groups - 1)])
    crossing = [(p * groups + g, (1 - p) * groups + g + 1) for p in range(planes) for g in range(groups - 1)]
    twin_before = lax.ppermute(edge, ("z_hi", "lags"), crossing)
    aside = lax.ppermute(jnp.concatenate([inverse, incident[0]], axis=0), "z_hi", swap)
    twin_inverse, twin_incident = aside[:size], aside[size:]

    received = exchange(pack(table, history, twin, before, twin_before), PLANE)
    high, low, first_high, first_low = split_kernel(kernel[0])
    partial0, partial1 = near_partial(near_t, base, received, high, low, planes * groups)

    partials = exchange(partial0, ("z_hi", "lags"))
    density0 = first_density(base, partials, incident, twin_incident, inverse, twin_inverse, chips, peers)
    mine = exchange(density0, ("y", "x"))
    partner = lax.ppermute(mine, "core", swap)

    driven = incident[1] - partial1
    for group in range(1, groups):
        driven = driven - lax.ppermute(partial1, "lags", [(group, 0)])

    density1 = last_density(near_t, base, core, mine, partner, first_high, first_low, driven, inverse)
    result = jnp.where(lax.axis_index("lags") == 0, density1, 0.0)
    for group in range(1, groups):
        result = result + lax.ppermute(density1, "lags", [(0, group)])
    return jnp.stack([density0[0, 0], result])


def solution(mesh):
    shape = (2, 4, 4, 2, mesh.shape["lags"])
    parts = Mesh(mesh.devices.reshape(shape), ROWS + ("lags",))
    in_specs = (
        P("lags", None, ROWS),
        P(None, None, ROWS),
        P(ROWS, "lags", None, None, None),
        P(ROWS, "lags", None),
        P(ROWS, None, None),
    )
    out_specs = P(None, None, ROWS)
    return jax.shard_map(shards, mesh=parts, in_specs=in_specs, out_specs=out_specs, check_vma=False)
```

time: 152 us -> 127 us (0.84)
  waiting for transfers between devices: 48.3 us -> 25.5 us
  Pallas kernels: 26.7 us -> 8.54 us
  blocking collectives: 13.5 us -> 29.5 us
  local copies, waits for them, and re-layouts: 12.5 us -> 22.9 us
  starting transfers between devices: 44.6 us -> 37.4 us
  other arithmetic: 4.27 us -> 1.36 us
    all_to_all x4 -> x2, waiting for transfers between devices: 36.4 us -> 17.9 us  [exchange(): return lax.all_to_all(array, axes, 0, 0, tiled=True)]
    pallas_call x6, Pallas kernels: 26.7 us -> 8.54 us  [the longest x5 6.28 us: call(): pl.pallas_call(body, out_shape=out, in_specs=in_specs, out_specs=jax.tree...]
    unnamed x24 -> x30, local copies, waits for them, and re-layouts: 5.03 us -> 22.2 us
    all_to_all x1 -> x2, blocking collectives: 13.5 us -> 29.5 us  [exchange(): return lax.all_to_all(array, axes, 0, 0, tiled=True)]
    all_to_all x4 -> x2, starting transfers between devices: 19.5 us -> 11.8 us  [exchange(): return lax.all_to_all(array, axes, 0, 0, tiled=True)]
    ppermute x4, waiting for transfers between devices: 4.49 us -> 0.01 us  [the longest x1 0.01 us: shards(): before = lax.ppermute(edge, 'lags', [(g, g + 1) for g in range(groups - 1)])]
    squeeze x3 -> x1, local copies, waits for them, and re-layouts: 4.09 us -> 0.75 us  [shards(): edge = history[lag_dev - 1]]
    broadcast_in_dim x4 -> x0, local copies, waits for them, and re-layouts: 3.15 us -> none  [the longest x1 1.7 us: shards(): spread = jnp.broadcast_to(density0[None], (chips, planes, waves, size))]
  transfers between devices with their start and end apart: 15 -> 13, of which waited for: 10 -> 7; matrix products, arithmetic and copies ran while one was open for 5% -> 1% of each run, Pallas kernels for 13% -> 5%
where the time goes in v2:
time: 127 us; the launch traced here: 125 us
  starting transfers between devices  37.4 us (29%)
  blocking collectives  29.5 us (23%)
  waiting for transfers between devices  25.5 us (20%)
  local copies, waits for them, and re-layouts  22.9 us (18%)
  Pallas kernels  8.54 us (7%)
  other arithmetic  1.36 us (1%)
    all_to_all x2, blocking collectives, exchange(): return lax.all_to_all(array, axes, 0, 0, tiled=True)  29.5 us
    unnamed x30, local copies, waits for them, and re-layouts  22.2 us
    all_to_all x2, waiting for transfers between devices, exchange(): return lax.all_to_all(array, axes, 0, 0, tiled=True)  17.9 us
    all_to_all x2, starting transfers between devices, exchange(): return lax.all_to_all(array, axes, 0, 0, tiled=True)  11.8 us
    ppermute x1, starting transfers between devices, shards(): twin = lax.ppermute(history, 'z_hi', swap)  7.19 us
    pallas_call x5, Pallas kernels, call(): pl.pallas_call(body, out_shape=out, in_specs=in_specs, out_specs=jax.tree...  6.28 us
    ppermute x3, waiting for transfers between devices, shards(): driven = driven - lax.ppermute(partial1, 'lags', [(group, 0)])  6.12 us
    ppermute x1, starting transfers between devices, shards(): lax.ppermute(jnp.concatenate([inverse, incident[0]], axis=0), 'z_hi', swap)  5.39 us
  transfers between devices with their start and end apart: 13, of which 7 were waited for; matrix products, arithmetic and copies ran while one was open for 1% of the time, Pallas kernels for 5%

profile of v2, /device:TPU:2, one launch (start us, length us, event | category | flops | bytes accessed | tf_op | source)
XLA Modules:
  0.0 125.4 jit_solution(18125279445610501450)
XLA Ops:
  0.0 7.2 %collective-permute-start = (f32[8,16,256]{2,1,0:T(8,128)}, f32[8,16,256]{2,1,0:T(8,128)S(1)}, u32[]{:S(2)}, u32[]{:S(2)}) collective-permute-start(f32[8,16,256]{2,1,0:T(8,128)} %own_ref.1), channel_id=1, source_target_pairs={{0,128},{128,0},{1,129},{129,1},{2,130},{130,2},{3,131},{131,3},{4... | collective-permute-start | bytes 393224 | tf_op jit(solution)/shard_map/ppermute | solution.py:192
  7.9 2.9 %collective-permute-start.1 = (f32[16,256]{1,0:T(8,128)S(1)}, f32[16,256]{1,0:T(8,128)S(1)}, u32[]{:S(2)}, u32[]{:S(2)}) collective-permute-start(f32[16,256]{1,0:T(8,128)S(1)} %slice_bitcast_fusion.2), channel_id=1, source_target_pairs={{0,1},{1,2},{2,3},{4,5},{5,6},{6,7},{8,9},{9,10},{10,11},{12,13},{... | collective-permute-start | bytes 49160 | tf_op jit(solution)/shard_map/ppermute | solution.py:195
  10.9 2.0 %collective-permute-start.2 = (f32[16,256]{1,0:T(8,128)S(1)}, f32[16,256]{1,0:T(8,128)S(1)}, u32[]{:S(2)}, u32[]{:S(2)}) collective-permute-start(f32[16,256]{1,0:T(8,128)S(1)} %slice_bitcast_fusion.2), channel_id=1, source_target_pairs={{0,129},{1,130},{2,131},{128,1},{129,2},{130,3},{4,133},{5,134},{6... | collective-permute-start | bytes 49160 | tf_op jit(solution)/shard_map/ppermute | solution.py:197
  14.2 13.6 %all_to_all.20.table_ref = s32[32,1,128]{2,1,0:T(1,128)S(1)} all-to-all(s32[32,1,128]{2,1,0:T(1,128)S(1)} %bitcast.26), channel_id=1, replica_groups=mesh['z_hi'=2,'y'=4,'x'=4,'core'=2,'lags'=4] {'y','x','core'}, dimensions={0} | all-to-all | bytes 32768 | tf_op jit(solution)/shard_map/all_to_all | solution.py:188
  28.7 1.0 shard_map.56
  29.8 1.3 %copy-done.1 = f32[32,2,2,16,256]{4,3,2,1,0:T(8,128)} copy-done((f32[32,2,2,16,256]{4,3,2,1,0:T(8,128)}, f32[32,2,2,16,256]{4,3,2,1,0:T(8,128)S(1)}, u32[]{:S(2)}) %copy-start.1) | copy-done | bytes 2097176
  31.1 5.1 %all-to-all-start.1 = ((f32[32,2,2,16,256]{4,3,2,1,0:T(8,128)}), f32[32,2,2,16,256]{4,3,2,1,0:T(8,128)S(1)}, u32[]{:S(2)}, u32[]{:S(2)}) async-start(f32[32,2,2,16,256]{4,3,2,1,0:T(8,128)} %copy-done.1), calls=%async_computation.1 | async-start | bytes 4194304 | tf_op jit(solution)/shard_map/all_to_all | solution.py:188
  36.9 5.4 %collective-permute-start.3 = (f32[272,256]{1,0:T(8,128)}, f32[272,256]{1,0:T(8,128)S(1)}, u32[]{:S(2)}, u32[]{:S(2)}) collective-permute-start(f32[272,256]{1,0:T(8,128)} %pad_maximum_fusion), channel_id=1, source_target_pairs={{0,128},{128,0},{1,129},{129,1},{2,130},{130,2},{3,131},{131,3},{4... | collective-permute-start | bytes 835592 | tf_op jit(solution)/shard_map/ppermute | solution.py:198
  42.3 4.6 %copy-done = f32[1,8,6,256,256]{4,3,2,1,0:T(8,128)S(1)} copy-done((f32[1,8,6,256,256]{4,3,2,1,0:T(8,128)S(1)}, f32[1,8,6,256,256]{4,3,2,1,0:T(8,128)}, u32[]{:S(2)}) %copy-start) | copy-done | bytes 12582936
  46.9 2.3 %split_kernel.1 = (bf16[8,6,256,256]{3,2,1,0:T(8,128)(2,1)S(1)}, bf16[8,6,256,256]{3,2,1,0:T(8,128)(2,1)S(1)}, bf16[6,256,256]{2,1,0:T(8,128)(2,1)S(1)}, bf16[6,256,256]{2,1,0:T(8,128)(2,1)S(1)}) custom-call(f32[8,6,256,256]{3,2,1,0:T(8,128)S(1)} %bitcast.22), custom_call_target="tpu_custom_call" | custom-call | tf_op jit(solution)/shard_map/split_kernel/pallas_call | solution.py:99
  49.2 2.6 %copy-done.2 = bf16[8,6,256,256]{3,2,1,0:T(8,128)(2,1)} copy-done((bf16[8,6,256,256]{3,2,1,0:T(8,128)(2,1)}, bf16[8,6,256,256]{3,2,1,0:T(8,128)(2,1)S(1)}, u32[]{:S(2)}) %copy-start.2) | copy-done | bytes 6291480
  51.8 2.6 %copy-done.4 = bf16[8,6,256,256]{3,2,1,0:T(8,128)(2,1)} copy-done((bf16[8,6,256,256]{3,2,1,0:T(8,128)(2,1)}, bf16[8,6,256,256]{3,2,1,0:T(8,128)(2,1)S(1)}, u32[]{:S(2)}) %copy-start.4) | copy-done | bytes 6291480
  55.3 8.9 %all-to-all-done.1.received_ref = f32[32,2,2,16,256]{4,3,2,1,0:T(8,128)S(1)} async-done(((f32[32,2,2,16,256]{4,3,2,1,0:T(8,128)}), f32[32,2,2,16,256]{4,3,2,1,0:T(8,128)S(1)}, u32[]{:S(2)}, u32[]{:S(2)}) %all-to-all-start.1) | async-done | bytes 2097184 | tf_op jit(solution)/shard_map/all_to_all | solution.py:188
  64.2 2.8 %copy-done.3 = bf16[8,6,256,256]{3,2,1,0:T(8,128)(2,1)S(1)} copy-done((bf16[8,6,256,256]{3,2,1,0:T(8,128)(2,1)S(1)}, bf16[8,6,256,256]{3,2,1,0:T(8,128)(2,1)}, u32[]{:S(2)}) %copy-start.3) | copy-done | bytes 6291480
  67.0 2.8 %copy-done.5 = bf16[8,6,256,256]{3,2,1,0:T(8,128)(2,1)S(1)} copy-done((bf16[8,6,256,256]{3,2,1,0:T(8,128)(2,1)S(1)}, bf16[8,6,256,256]{3,2,1,0:T(8,128)(2,1)}, u32[]{:S(2)}) %copy-start.5) | copy-done | bytes 6291480
  69.8 3.3 %shard_map.57 = (f32[8,16,256]{2,1,0:T(8,128)}, f32[16,256]{1,0:T(8,128)S(1)}) custom-call(s32[6,1,8]{2,1,0:T(1,128)S(1)} %bitcast.28, s32[1]{0:T(128)} %bitcast.base_ref, f32[32,2,2,16,256]{4,3,2,1,0:T(8,128)S(1)} %all-to-all-done.1.received_ref, bf16[8,6,256,256]{3,2,1,0:T(8,128)(2,1)S(1)} %copy-done.3, bf16[8,6,256,256]{3,2,1,0:T(8,128)(2,1)S(1)} %copy-done.5), custom_call_target="tpu_custom_call" | custom-call | tf_op jit(solution)/shard_map/pallas_call | solution.py:25
  73.1 6.7 %all-to-all-start.2 = ((f32[8,16,256]{2,1,0:T(8,128)}), f32[8,16,256]{2,1,0:T(8,128)S(1)}, u32[]{:S(2)}, u32[]{:S(2)}) async-start(f32[8,16,256]{2,1,0:T(8,128)} %get-tuple-element.13), calls=%async_computation.2 | async-start | bytes 262144 | tf_op jit(solution)/shard_map/all_to_all | solution.py:188
  79.8 9.0 %all-to-all-done.2.partials_ref = f32[8,16,256]{2,1,0:T(8,128)S(1)} async-done(((f32[8,16,256]{2,1,0:T(8,128)}), f32[8,16,256]{2,1,0:T(8,128)S(1)}, u32[]{:S(2)}, u32[]{:S(2)}) %all-to-all-start.2) | async-done | bytes 131104 | tf_op jit(solution)/shard_map/all_to_all | solution.py:188
  89.1 15.9 %all_to_all.21.mine_ref = f32[16,2,16,256]{3,2,1,0:T(8,128)S(1)} all-to-all(f32[16,2,16,256]{3,2,1,0:T(8,128)S(1)} %shard_map.58), channel_id=1, replica_groups=mesh['z_hi'=2,'y'=4,'x'=4,'core'=2,'lags'=4] {'y','x'}, dimensions={0} | all-to-all | bytes 1048576 | tf_op jit(solution)/shard_map/all_to_all | solution.py:188
  105.0 1.3 %collective-permute-start.5 = (f32[16,256]{1,0:T(8,128)S(1)}, f32[16,256]{1,0:T(8,128)S(1)}, u32[]{:S(2)}, u32[]{:S(2)}) collective-permute-start(f32[16,256]{1,0:T(8,128)S(1)} %get-tuple-element.16), channel_id=1, source_target_pairs={{1,0},{5,4},{9,8},{13,12},{17,16},{21,20},{25,24},{29,28},{33,32},... | collective-permute-start | bytes 49160 | tf_op jit(solution)/shard_map/ppermute | solution.py:212
  106.3 1.3 %collective-permute-start.6 = (f32[16,256]{1,0:T(8,128)S(1)}, f32[16,256]{1,0:T(8,128)S(1)}, u32[]{:S(2)}, u32[]{:S(2)}) collective-permute-start(f32[16,256]{1,0:T(8,128)S(1)} %get-tuple-element.16), channel_id=1, source_target_pairs={{2,0},{6,4},{10,8},{14,12},{18,16},{22,20},{26,24},{30,28},{34,32}... | collective-permute-start | bytes 49160 | tf_op jit(solution)/shard_map/ppermute | solution.py:212
  107.6 1.3 %collective-permute-start.7 = (f32[16,256]{1,0:T(8,128)S(1)}, f32[16,256]{1,0:T(8,128)S(1)}, u32[]{:S(2)}, u32[]{:S(2)}) collective-permute-start(f32[16,256]{1,0:T(8,128)S(1)} %get-tuple-element.16), channel_id=1, source_target_pairs={{3,0},{7,4},{11,8},{15,12},{19,16},{23,20},{27,24},{31,28},{35,32}... | collective-permute-start | bytes 49160 | tf_op jit(solution)/shard_map/ppermute | solution.py:212
  108.9 1.7 %collective-permute-done.5 = f32[16,256]{1,0:T(8,128)S(1)} collective-permute-done((f32[16,256]{1,0:T(8,128)S(1)}, f32[16,256]{1,0:T(8,128)S(1)}, u32[]{:S(2)}, u32[]{:S(2)}) %collective-permute-start.5) | collective-permute-done | bytes 16416 | tf_op jit(solution)/shard_map/ppermute | solution.py:212
  110.6 2.2 %collective-permute-done.6 = f32[16,256]{1,0:T(8,128)S(1)} collective-permute-done((f32[16,256]{1,0:T(8,128)S(1)}, f32[16,256]{1,0:T(8,128)S(1)}, u32[]{:S(2)}, u32[]{:S(2)}) %collective-permute-start.6) | collective-permute-done | bytes 16416 | tf_op jit(solution)/shard_map/ppermute | solution.py:212
  112.8 2.2 %collective-permute-done.7 = f32[16,256]{1,0:T(8,128)S(1)} collective-permute-done((f32[16,256]{1,0:T(8,128)S(1)}, f32[16,256]{1,0:T(8,128)S(1)}, u32[]{:S(2)}, u32[]{:S(2)}) %collective-permute-start.7) | collective-permute-done | bytes 16416 | tf_op jit(solution)/shard_map/ppermute | solution.py:212
  115.8 1.1 copy-done.8
  117.0 1.0 copy-done.10
  118.0 1.1 shard_map.59
  119.1 1.6 %collective-permute-start.10 = (f32[16,256]{1,0:T(8,128)S(1)}, f32[16,256]{1,0:T(8,128)S(1)}, u32[]{:S(2)}, u32[]{:S(2)}) collective-permute-start(f32[16,256]{1,0:T(8,128)S(1)} %shard_map.59), channel_id=1, source_target_pairs={{0,3},{4,7},{8,11},{12,15},{16,19},{20,23},{24,27},{28,31},{32,35}... | collective-permute-start | bytes 49160 | tf_op jit(solution)/shard_map/ppermute | solution.py:217
  120.7 1.3 %collective-permute-start.8 = (f32[16,256]{1,0:T(8,128)S(1)}, f32[16,256]{1,0:T(8,128)S(1)}, u32[]{:S(2)}, u32[]{:S(2)}) collective-permute-start(f32[16,256]{1,0:T(8,128)S(1)} %shard_map.59), channel_id=1, source_target_pairs={{0,1},{4,5},{8,9},{12,13},{16,17},{20,21},{24,25},{28,29},{32,33},... | collective-permute-start | bytes 49160 | tf_op jit(solution)/shard_map/ppermute | solution.py:217
  122.0 1.3 %collective-permute-start.9 = (f32[16,256]{1,0:T(8,128)S(1)}, f32[16,256]{1,0:T(8,128)S(1)}, u32[]{:S(2)}, u32[]{:S(2)}) collective-permute-start(f32[16,256]{1,0:T(8,128)S(1)} %shard_map.59), channel_id=1, source_target_pairs={{0,2},{4,6},{8,10},{12,14},{16,18},{20,22},{24,26},{28,30},{32,34}... | collective-permute-start | bytes 49160 | tf_op jit(solution)/shard_map/ppermute | solution.py:217
  123.4 1.3 %collective-permute-done.9 = f32[16,256]{1,0:T(8,128)S(1)} collective-permute-done((f32[16,256]{1,0:T(8,128)S(1)}, f32[16,256]{1,0:T(8,128)S(1)}, u32[]{:S(2)}, u32[]{:S(2)}) %collective-permute-start.9) | collective-permute-done | bytes 16416 | tf_op jit(solution)/shard_map/ppermute | solution.py:217
  (41 shorter events, 6.5 us)
Async XLA Ops:
  0.0 36.2 %copy-start.6 = (f32[1,256,256]{2,1,0:T(8,128)S(1)}, f32[1,256,256]{2,1,0:T(8,128)}, u32[]{:S(2)}) copy-start(f32[1,256,256]{2,1,0:T(8,128)} %param.9) | copy-start | bytes 786436
  0.0 27.8 %collective-permute-start = (f32[8,16,256]{2,1,0:T(8,128)}, f32[8,16,256]{2,1,0:T(8,128)S(1)}, u32[]{:S(2)}, u32[]{:S(2)}) collective-permute-start(f32[8,16,256]{2,1,0:T(8,128)} %own_ref.1), channel_id=1, source_target_pairs={{0,128},{128,0},{1,129},{129,1},{2,130},{130,2},{3,131},{131,3},{4... | collective-permute-start | bytes 393224 | tf_op jit(solution)/shard_map/ppermute | solution.py:192
  7.9 19.9 %collective-permute-start.1 = (f32[16,256]{1,0:T(8,128)S(1)}, f32[16,256]{1,0:T(8,128)S(1)}, u32[]{:S(2)}, u32[]{:S(2)}) collective-permute-start(f32[16,256]{1,0:T(8,128)S(1)} %slice_bitcast_fusion.2), channel_id=1, source_target_pairs={{0,1},{1,2},{2,3},{4,5},{5,6},{6,7},{8,9},{9,10},{10,11},{12,13},{... | collective-permute-start | bytes 49160 | tf_op jit(solution)/shard_map/ppermute | solution.py:195
  10.9 17.0 %collective-permute-start.2 = (f32[16,256]{1,0:T(8,128)S(1)}, f32[16,256]{1,0:T(8,128)S(1)}, u32[]{:S(2)}, u32[]{:S(2)}) collective-permute-start(f32[16,256]{1,0:T(8,128)S(1)} %slice_bitcast_fusion.2), channel_id=1, source_target_pairs={{0,129},{1,130},{2,131},{128,1},{129,2},{130,3},{4,133},{5,134},{6... | collective-permute-start | bytes 49160 | tf_op jit(solution)/shard_map/ppermute | solution.py:197
  12.9 0.7 copy-start.13
  27.8 0.9 copy-start.11
  28.7 7.4 %copy-start.12 = (f32[2,16,256]{2,1,0:T(8,128)S(1)}, f32[2,16,256]{2,1,0:T(8,128)}, u32[]{:S(2)}) copy-start(f32[2,16,256]{2,1,0:T(8,128)} %inc_ref.1) | copy-start | bytes 98308
  29.8 1.3 %copy-start.1 = (f32[32,2,2,16,256]{4,3,2,1,0:T(8,128)}, f32[32,2,2,16,256]{4,3,2,1,0:T(8,128)S(1)}, u32[]{:S(2)}) copy-start(f32[32,2,2,16,256]{4,3,2,1,0:T(8,128)S(1)} %shard_map.56) | copy-start | bytes 6291460
  31.1 33.1 %all-to-all-start.1 = ((f32[32,2,2,16,256]{4,3,2,1,0:T(8,128)}), f32[32,2,2,16,256]{4,3,2,1,0:T(8,128)S(1)}, u32[]{:S(2)}, u32[]{:S(2)}) async-start(f32[32,2,2,16,256]{4,3,2,1,0:T(8,128)} %copy-done.1), calls=%async_computation.1 | async-start | bytes 4194304 | tf_op jit(solution)/shard_map/all_to_all | solution.py:188
  36.9 42.8 %collective-permute-start.3 = (f32[272,256]{1,0:T(8,128)}, f32[272,256]{1,0:T(8,128)S(1)}, u32[]{:S(2)}, u32[]{:S(2)}) collective-permute-start(f32[272,256]{1,0:T(8,128)} %pad_maximum_fusion), channel_id=1, source_target_pairs={{0,128},{128,0},{1,129},{129,1},{2,130},{130,2},{3,131},{131,3},{4... | collective-permute-start | bytes 835592 | tf_op jit(solution)/shard_map/ppermute | solution.py:198
  42.3 4.6 %copy-start = (f32[1,8,6,256,256]{4,3,2,1,0:T(8,128)S(1)}, f32[1,8,6,256,256]{4,3,2,1,0:T(8,128)}, u32[]{:S(2)}) copy-start(f32[1,8,6,256,256]{4,3,2,1,0:T(8,128)} %param.7) | copy-start | bytes 37748740
  46.9 17.3 %copy-start.14 = (s32[1,8,6]{1,0,2:T(1,128)S(1)}, s32[1,8,6]{1,0,2:T(1,128)}, u32[]{:S(2)}) copy-start(s32[1,8,6]{1,0,2:T(1,128)} %param.8) | copy-start | bytes 580
  49.2 2.6 %copy-start.2 = (bf16[8,6,256,256]{3,2,1,0:T(8,128)(2,1)}, bf16[8,6,256,256]{3,2,1,0:T(8,128)(2,1)S(1)}, u32[]{:S(2)}) copy-start(bf16[8,6,256,256]{3,2,1,0:T(8,128)(2,1)S(1)} %get-tuple-element.11.high_ref) | copy-start | bytes 18874372
  51.8 2.6 %copy-start.4 = (bf16[8,6,256,256]{3,2,1,0:T(8,128)(2,1)}, bf16[8,6,256,256]{3,2,1,0:T(8,128)(2,1)S(1)}, u32[]{:S(2)}) copy-start(bf16[8,6,256,256]{3,2,1,0:T(8,128)(2,1)S(1)} %get-tuple-element.12.low_ref) | copy-start | bytes 18874372
  54.4 0.9 copy-start.7
  64.2 2.8 %copy-start.3 = (bf16[8,6,256,256]{3,2,1,0:T(8,128)(2,1)S(1)}, bf16[8,6,256,256]{3,2,1,0:T(8,128)(2,1)}, u32[]{:S(2)}) copy-start(bf16[8,6,256,256]{3,2,1,0:T(8,128)(2,1)} %copy-done.2) | copy-start | bytes 18874372
  67.0 2.8 %copy-start.5 = (bf16[8,6,256,256]{3,2,1,0:T(8,128)(2,1)S(1)}, bf16[8,6,256,256]{3,2,1,0:T(8,128)(2,1)}, u32[]{:S(2)}) copy-start(bf16[8,6,256,256]{3,2,1,0:T(8,128)(2,1)} %copy-done.4) | copy-start | bytes 18874372
  73.1 15.7 %all-to-all-start.2 = ((f32[8,16,256]{2,1,0:T(8,128)}), f32[8,16,256]{2,1,0:T(8,128)S(1)}, u32[]{:S(2)}, u32[]{:S(2)}) async-start(f32[8,16,256]{2,1,0:T(8,128)} %get-tuple-element.13), calls=%async_computation.2 | async-start | bytes 262144 | tf_op jit(solution)/shard_map/all_to_all | solution.py:188
  105.0 10.0 %collective-permute-start.4 = (f32[16,2,16,256]{3,2,1,0:T(8,128)S(1)}, f32[16,2,16,256]{3,2,1,0:T(8,128)S(1)}, u32[]{:S(2)}, u32[]{:S(2)}) collective-permute-start(f32[16,2,16,256]{3,2,1,0:T(8,128)S(1)} %all_to_all.21.mine_ref), channel_id=1, source_target_pairs={{0,4},{4,0},{1,5},{5,1},{2,6},{6,2},{3,7},{7,3},{8,12},{12,8},{9,1... | collective-permute-start | bytes 1572872 | tf_op jit(solution)/shard_map/ppermute | solution.py:208
  105.0 5.6 %collective-permute-start.5 = (f32[16,256]{1,0:T(8,128)S(1)}, f32[16,256]{1,0:T(8,128)S(1)}, u32[]{:S(2)}, u32[]{:S(2)}) collective-permute-start(f32[16,256]{1,0:T(8,128)S(1)} %get-tuple-element.16), channel_id=1, source_target_pairs={{1,0},{5,4},{9,8},{13,12},{17,16},{21,20},{25,24},{29,28},{33,32},... | collective-permute-start | bytes 49160 | tf_op jit(solution)/shard_map/ppermute | solution.py:212
  106.3 6.5 %collective-permute-start.6 = (f32[16,256]{1,0:T(8,128)S(1)}, f32[16,256]{1,0:T(8,128)S(1)}, u32[]{:S(2)}, u32[]{:S(2)}) collective-permute-start(f32[16,256]{1,0:T(8,128)S(1)} %get-tuple-element.16), channel_id=1, source_target_pairs={{2,0},{6,4},{10,8},{14,12},{18,16},{22,20},{26,24},{30,28},{34,32}... | collective-permute-start | bytes 49160 | tf_op jit(solution)/shard_map/ppermute | solution.py:212
  107.6 7.4 %collective-permute-start.7 = (f32[16,256]{1,0:T(8,128)S(1)}, f32[16,256]{1,0:T(8,128)S(1)}, u32[]{:S(2)}, u32[]{:S(2)}) collective-permute-start(f32[16,256]{1,0:T(8,128)S(1)} %get-tuple-element.16), channel_id=1, source_target_pairs={{3,0},{7,4},{11,8},{15,12},{19,16},{23,20},{27,24},{31,28},{35,32}... | collective-permute-start | bytes 49160 | tf_op jit(solution)/shard_map/ppermute | solution.py:212
  115.0 0.8 copy-start.9
  115.8 1.1 copy-start.8
  117.0 1.0 copy-start.10
  119.1 4.2 %collective-permute-start.10 = (f32[16,256]{1,0:T(8,128)S(1)}, f32[16,256]{1,0:T(8,128)S(1)}, u32[]{:S(2)}, u32[]{:S(2)}) collective-permute-start(f32[16,256]{1,0:T(8,128)S(1)} %shard_map.59), channel_id=1, source_target_pairs={{0,3},{4,7},{8,11},{12,15},{16,19},{20,23},{24,27},{28,31},{32,35}... | collective-permute-start | bytes 49160 | tf_op jit(solution)/shard_map/ppermute | solution.py:217
  120.7 2.7 %collective-permute-start.8 = (f32[16,256]{1,0:T(8,128)S(1)}, f32[16,256]{1,0:T(8,128)S(1)}, u32[]{:S(2)}, u32[]{:S(2)}) collective-permute-start(f32[16,256]{1,0:T(8,128)S(1)} %shard_map.59), channel_id=1, source_target_pairs={{0,1},{4,5},{8,9},{12,13},{16,17},{20,21},{24,25},{28,29},{32,33},... | collective-permute-start | bytes 49160 | tf_op jit(solution)/shard_map/ppermute | solution.py:217
  122.0 2.7 %collective-permute-start.9 = (f32[16,256]{1,0:T(8,128)S(1)}, f32[16,256]{1,0:T(8,128)S(1)}, u32[]{:S(2)}, u32[]{:S(2)}) collective-permute-start(f32[16,256]{1,0:T(8,128)S(1)} %shard_map.59), channel_id=1, source_target_pairs={{0,2},{4,6},{8,10},{12,14},{16,18},{20,22},{24,26},{28,30},{32,34}... | collective-permute-start | bytes 49160 | tf_op jit(solution)/shard_map/ppermute | solution.py:217

commit v3 on v2

v3 whole, which is shorter than its diff:
```python
import jax
import jax.numpy as jnp
from jax import lax
from jax.experimental import pallas as pl
from jax.experimental.pallas import tpu as pltpu
from jax.sharding import Mesh
from jax.sharding import PartitionSpec as P


PLANE = ("y", "x", "core")
ROWS = ("z_hi",) + PLANE
F32 = jnp.float32
BF16 = jnp.bfloat16
VMEM = pl.BlockSpec(memory_space=pltpu.VMEM)
SMEM = pl.BlockSpec(memory_space=pltpu.SMEM)
PARAMS = pltpu.CompilerParams(vmem_limit_bytes=8 << 20)


def resident(array):
    return pltpu.with_memory_space_constraint(array, pltpu.VMEM)


def call(body, out, in_specs, operands, aliases=None):
    held = [resident(a) if s is VMEM else a for a, s in zip(operands, in_specs)]
    return pl.pallas_call(
        body,
        out_shape=out,
        in_specs=in_specs,
        out_specs=jax.tree.map(lambda _: VMEM, out),
        input_output_aliases=aliases or {},
        compiler_params=PARAMS,
    )(*held)


def split(value):
    high = value.astype(BF16)
    low = (value - high.astype(F32)).astype(BF16)
    return high, low


def product(left, right_high, right_low):
    waves = left.shape[0]
    left_high, left_low = split(left)
    both = jnp.concatenate([left_high, left_low], axis=0)
    first = jnp.dot(both, right_high, preferred_element_type=F32)
    second = jnp.dot(left_high, right_low, preferred_element_type=F32)
    return first[:waves] + (first[waves:] + second)


def lag_table(near_t, place, peers, lanes):
    near, _, lag_dev = near_t.shape

    def body(near_ref, place_ref, out_ref):
        ids = lax.broadcasted_iota(jnp.int32, (peers, lanes), 1) * peers
        ids = ids + lax.broadcasted_iota(jnp.int32, (peers, lanes), 0)
        table = jnp.zeros((peers, lanes), jnp.int32)
        for slot in range(near):
            for lag in range(1, lag_dev):
                source = jnp.bitwise_xor(near_ref[slot, 0, lag], place_ref[0])
                table = jnp.where(ids == source, lag, table)
        out_ref[...] = table

    return call(body, jax.ShapeDtypeStruct((peers, lanes), jnp.int32), [SMEM, SMEM], [near_t, place])


def stage(history):
    def body(history_ref, out_ref):
        out_ref[...] = history_ref[...]

    return pl.pallas_call(
        body,
        out_shape=pltpu.VMEM(history.shape, F32),
        out_specs=VMEM,
        compiler_params=PARAMS,
        name="stage",
    )(pltpu.with_memory_space_constraint(history, pltpu.HBM))


def pack(table, own, twin):
    peers, _, _ = table.shape
    block = own.shape[1:]
    part = peers // 4

    def body(table_ref, own_ref, twin_ref, out_ref):
        for step in range(part):
            peer = pl.program_id(0) * part + step
            for plane, ref in enumerate((own_ref, twin_ref)):
                lag = table_ref[peer, 0, plane]
                out_ref[step, 0, plane] = ref[lag]
                out_ref[step, 1, plane] = ref[jnp.maximum(lag - 1, 0)]

    return pl.pallas_call(
        body,
        grid=(peers // part,),
        out_shape=pltpu.HBM((peers, 2, 2) + block, F32),
        in_specs=[SMEM, VMEM, VMEM],
        out_specs=pl.BlockSpec((part, 2, 2) + block, lambda step: (step, 0, 0, 0, 0)),
        compiler_params=PARAMS,
        name="pack",
    )(table, resident(own), resident(twin))


def split_kernel(kernel):
    lag_dev, near, size, _ = kernel.shape

    def body(kernel_ref, high_ref, low_ref):
        high, low = split(kernel_ref[0])
        high_ref[0] = high
        low_ref[0] = low

    spec = pl.BlockSpec((1, near, size, size), lambda lag: (lag, 0, 0, 0))
    out = pltpu.HBM(kernel.shape, BF16)
    return pl.pallas_call(
        body,
        grid=(lag_dev,),
        out_shape=(out, out),
        in_specs=[spec],
        out_specs=(spec, spec),
        compiler_params=PARAMS,
        name="split_kernel",
    )(pltpu.with_memory_space_constraint(kernel, pltpu.HBM))


def near_partial(near_t, place, received, high, low, copies):
    lag_dev, near, size, _ = high.shape
    peers, steps, _, waves, _ = received.shape

    def body(near_ref, place_ref, received_ref, high_ref, low_ref, out_ref, rest_ref, total_ref):
        lag = pl.program_id(0)
        total = jnp.zeros((steps * waves, size), F32)
        for slot in range(near):
            source = jnp.bitwise_xor(near_ref[slot, 0, lag], place_ref[0])
            peer, plane = source % peers, source // peers
            later = jnp.where(lag == 0, 0.0, received_ref[peer, 1, plane])
            block = jnp.concatenate([received_ref[peer, 0, plane], later], axis=0)
            total = total + product(block, high_ref[0, slot], low_ref[0, slot])

        @pl.when(lag == 0)
        def _():
            total_ref[...] = total

        @pl.when(lag > 0)
        def _():
            total_ref[...] += total

        @pl.when(lag == lag_dev - 1)
        def _():
            for copy in range(copies):
                out_ref[copy] = total_ref[:waves]
            rest_ref[...] = total_ref[waves:]

    spec = pl.BlockSpec((1, near, size, size), lambda lag: (lag, 0, 0, 0))
    return pl.pallas_call(
        body,
        grid=(lag_dev,),
        out_shape=(
            jax.ShapeDtypeStruct((copies, waves, size), F32),
            jax.ShapeDtypeStruct((waves, size), F32),
        ),
        in_specs=[SMEM, SMEM, VMEM, spec, spec],
        out_specs=(VMEM, VMEM),
        scratch_shapes=[pltpu.VMEM((steps * waves, size), F32)],
        compiler_params=PARAMS,
        name="near",
    )(
        near_t,
        place,
        resident(received),
        pltpu.with_memory_space_constraint(high, pltpu.HBM),
        pltpu.with_memory_space_constraint(low, pltpu.HBM),
    )


def gather_twin(aside, before, twin_before, incident):
    waves, size = before.shape

    def body(aside_ref, before_ref, twin_before_ref, incident_ref, pair_ref, inverse_ref):
        pair_ref[0, 0] = incident_ref[0]
        pair_ref[0, 1] = aside_ref[size:]
        pair_ref[1, 0] = before_ref[...]
        pair_ref[1, 1] = twin_before_ref[...]
        inverse_ref[...] = aside_ref[:size]

    out = (pltpu.VMEM((2, 2, waves, size), F32), pltpu.VMEM((size, size), F32))
    return call(body, out, [VMEM] * 4, [aside, before, twin_before, incident])


def first_density(place, partials, pair, inverse, twin_inverse, chips, peers):
    groups = partials.shape[0] // 2
    waves, size = partials.shape[1:]

    def body(place_ref, partials_ref, pair_ref, inv_ref, twin_inv_ref, density_ref, out_ref):
        own = (place_ref[0] // peers) * groups
        twin = groups - own
        near = partials_ref[own]
        twin_near = partials_ref[twin]
        for group in range(1, groups):
            near = near + partials_ref[own + group]
            twin_near = twin_near + partials_ref[twin + group]
        density = product(pair_ref[0, 0] - near, *split(inv_ref[...]))
        twin_density = product(pair_ref[0, 1] - twin_near, *split(twin_inv_ref[...]))
        density_ref[...] = density
        new = place_ref[2] == 0
        first = jnp.where(new, density, pair_ref[1, 0])
        second = jnp.where(new, twin_density, pair_ref[1, 1])
        for chip in range(chips):
            out_ref[chip, 0] = first
            out_ref[chip, 1] = second

    out = (pltpu.VMEM((waves, size), F32), pltpu.VMEM((chips, 2, waves, size), F32))
    operands = [place, partials, pair, inverse, twin_inverse]
    return call(body, out, [SMEM] + [VMEM] * 4, operands)


def first_lag(near_t, place, mine, partner, high, low, rest):
    near = near_t.shape[0]
    chips = mine.shape[0]

    def body(near_ref, place_ref, mine_ref, partner_ref, high_ref, low_ref, rest_ref, out_ref):
        total = rest_ref[...]
        for slot in range(near):
            source = jnp.bitwise_xor(near_ref[slot, 0, 0], place_ref[0])
            chip = (source // 2) % chips
            plane = source // (2 * chips)
            same = (source % 2) == place_ref[1]
            block = jnp.where(same, mine_ref[chip, plane], partner_ref[chip, plane])
            total = total + product(block, high_ref[0, slot], low_ref[0, slot])
        out_ref[...] = total

    first = pl.BlockSpec((1,) + high.shape[1:], lambda step: (0, 0, 0, 0))
    return pl.pallas_call(
        body,
        grid=(1,),
        out_shape=pltpu.VMEM(rest.shape, F32),
        in_specs=[SMEM, SMEM, VMEM, VMEM, first, first, VMEM],
        out_specs=VMEM,
        compiler_params=PARAMS,
        name="first_lag",
    )(
        near_t,
        place,
        resident(mine),
        resident(partner),
        pltpu.with_memory_space_constraint(high, pltpu.HBM),
        pltpu.with_memory_space_constraint(low, pltpu.HBM),
        resident(rest),
    )


def last_density(place, partials, incident, inverse, density0):
    groups = len(partials)

    def body(place_ref, inc_ref, inv_ref, density_ref, *refs):
        terms, (out_ref, held_ref) = refs[:groups], refs[groups:]
        for ahead, term in enumerate(terms):
            held_ref[lax.rem(place_ref[2] - ahead + groups, groups)] = term[...]
        driven = inc_ref[1]
        for group in range(groups):
            driven = driven - held_ref[group]
        out_ref[0] = density_ref[...]
        out_ref[1] = product(driven, *split(inv_ref[...]))

    operands = [incident, inverse, density0, *partials]
    return pl.pallas_call(
        body,
        out_shape=jax.ShapeDtypeStruct((2,) + density0.shape, F32),
        in_specs=[SMEM] + [VMEM] * len(operands),
        out_specs=VMEM,
        scratch_shapes=[pltpu.VMEM((groups,) + density0.shape, F32)],
        compiler_params=PARAMS,
        name="last_density",
    )(place, *[resident(a) for a in operands])


def shards(history, incident, kernel, near_blocks, self_inverse):
    lag_dev, _, _ = history.shape
    inverse = self_inverse[0]
    planes = lax.axis_size("z_hi")
    peers = lax.axis_size(PLANE)
    chips = peers // 2
    groups = lax.axis_size("lags")
    place = jnp.stack([lax.axis_index("z_hi") * peers, lax.axis_index("core"), lax.axis_index("lags")])
    near_t = jnp.transpose(near_blocks, (2, 0, 1))
    swap = [(0, 1), (1, 0)]

    def exchange(array, axes):
        return lax.all_to_all(array, axes, 0, 0, tiled=True)

    table = lag_table(near_t, place, peers, 128)
    table = exchange(table[:, None, :], PLANE)
    twin = lax.ppermute(history, "z_hi", swap)
    received = exchange(pack(table, stage(history), twin), PLANE)

    edge = history[lag_dev - 1]
    before = lax.ppermute(edge, "lags", [(g, g + 1) for g in range(groups - 1)])
    crossing = [(p * groups + g, (1 - p) * groups + g + 1) for p in range(planes) for g in range(groups - 1)]
    twin_before = lax.ppermute(edge, ("z_hi", "lags"), crossing)
    aside = lax.ppermute(jnp.concatenate([inverse, incident[0]], axis=0), "z_hi", swap)
    pair, twin_inverse = gather_twin(aside, before, twin_before, incident)

    high, low = split_kernel(kernel[0])
    partial0, partial1 = near_partial(near_t, place, received, high, low, planes * groups)

    partials = exchange(partial0, ("z_hi", "lags"))
    density0, spread = first_density(place, partials, pair, inverse, twin_inverse, chips, peers)
    mine = exchange(spread, ("y", "x"))
    partner = lax.ppermute(mine, "core", swap)

    partial1 = first_lag(near_t, place, mine, partner, high, low, partial1)
    terms = [partial1]
    for ahead in range(1, groups):
        route = [(g, (g + ahead) % groups) for g in range(groups)]
        terms.append(lax.ppermute(partial1, "lags", route))
    return last_density(place, terms, incident, inverse, density0)


def solution(mesh):
    shape = (2, 4, 4, 2, mesh.shape["lags"])
    parts = Mesh(mesh.devices.reshape(shape), ROWS + ("lags",))
    in_specs = (
        P("lags", None, ROWS),
        P(None, None, ROWS),
        P(ROWS, "lags", None, None, None),
        P(ROWS, "lags", None),
        P(ROWS, None, None),
    )
    out_specs = P(None, None, ROWS)
    return jax.shard_map(shards, mesh=parts, in_specs=in_specs, out_specs=out_specs, check_vma=False)
```

time: 127 us -> 112 us (0.88)
  local copies, waits for them, and re-layouts: 22.9 us -> 1.42 us
  Pallas kernels: 8.54 us -> 28.6 us
  blocking collectives: 29.5 us -> 14.3 us
  starting transfers between devices: 37.4 us -> 39.4 us
    pallas_call x1 -> x6, Pallas kernels: 2.26 us -> 26.6 us  [the longest x1 11.3 us: split_kernel(): pl.pallas_call(body, grid=(lag_dev,), out_shape=(out, out), in_specs=[spe...]
    unnamed x30 -> x8, local copies, waits for them, and re-layouts: 22.2 us -> 0.7 us
    all_to_all x2 -> x1, blocking collectives: 29.5 us -> 14.3 us  [exchange(): return lax.all_to_all(array, axes, 0, 0, tiled=True)]
    ppermute x6 -> x3, waiting for transfers between devices: 7.53 us -> 1.47 us  [shards(): terms.append(lax.ppermute(partial1, 'lags', route))]
    ppermute x1, starting transfers between devices: 5.39 us -> 0.1 us  [shards(): lax.ppermute(jnp.concatenate([inverse, incident[0]], axis=0), 'z_hi', swap)]
    all_to_all x2 -> x3, starting transfers between devices: 11.8 us -> 16.1 us  [exchange(): return lax.all_to_all(array, axes, 0, 0, tiled=True)]
    pallas_call x5 -> x3, Pallas kernels: 6.28 us -> 2.06 us  [call(): pl.pallas_call(body, out_shape=out, in_specs=in_specs, out_specs=jax.tree...]
    all_to_all x2 -> x3, waiting for transfers between devices: 17.9 us -> 21.7 us  [exchange(): return lax.all_to_all(array, axes, 0, 0, tiled=True)]
  transfers between devices with their start and end apart: 13 -> 11, of which waited for: 7 -> 5; matrix products, arithmetic and copies ran while one was open for 1% -> 1% of each run, Pallas kernels for 5% -> 20%
where the time goes in v3:
time: 112 us; the launch traced here: 110 us
  starting transfers between devices  39.4 us (35%)
  Pallas kernels  28.6 us (26%)
  waiting for transfers between devices  26.5 us (24%)
  blocking collectives  14.3 us (13%)
  local copies, waits for them, and re-layouts  1.42 us (1%)
    all_to_all x3, waiting for transfers between devices, exchange(): return lax.all_to_all(array, axes, 0, 0, tiled=True)  21.7 us
    all_to_all x3, starting transfers between devices, exchange(): return lax.all_to_all(array, axes, 0, 0, tiled=True)  16.1 us
    all_to_all x1, blocking collectives, exchange(): return lax.all_to_all(array, axes, 0, 0, tiled=True)  14.3 us
    pallas_call x1, Pallas kernels, split_kernel(): pl.pallas_call(body, grid=(lag_dev,), out_shape=(out, out), in_specs=[spe...  11.3 us
    pallas_call x1, Pallas kernels, near_partial(): pl.pallas_call(body, grid=(lag_dev,), out_shape=(jax.ShapeDtypeStruct((co...  8.55 us
    ppermute x1, starting transfers between devices, shards(): twin = lax.ppermute(history, 'z_hi', swap)  7.19 us
    ppermute x3, starting transfers between devices, shards(): terms.append(lax.ppermute(partial1, 'lags', route))  6.73 us
    ppermute x1, starting transfers between devices, shards(): twin_before = lax.ppermute(edge, ('z_hi', 'lags'), crossing)  5.51 us
  transfers between devices with their start and end apart: 11, of which 5 were waited for; matrix products, arithmetic and copies ran while one was open for 1% of the time, Pallas kernels for 20%

profile of v3, /device:TPU:2, one launch (start us, length us, event | category | flops | bytes accessed | tf_op | source)
XLA Modules:
  0.0 110.5 jit_solution(18245251634467093626)
XLA Ops:
  0.0 7.2 %collective-permute-start = (f32[8,16,256]{2,1,0:T(8,128)}, f32[8,16,256]{2,1,0:T(8,128)S(1)}, u32[]{:S(2)}, u32[]{:S(2)}) collective-permute-start(f32[8,16,256]{2,1,0:T(8,128)} %history_ref.1), channel_id=1, source_target_pairs={{0,128},{128,0},{1,129},{129,1},{2,130},{130,2},{3,131},{131,3},{4... | collective-permute-start | bytes 393224 | tf_op jit(solution)/shard_map/ppermute | solution.py:291
  7.2 0.1 pad_add_fusion.place_ref
  7.3 0.7 copy-done.2
  8.0 1.3 %shard_map.55 = s32[32,128]{1,0:T(8,128)} custom-call(s32[6,1,8]{2,1,0:T(1,128)S(1)} %bitcast.14, s32[3]{0:T(128)S(1)} %pad_add_fusion.place_ref), custom_call_target="tpu_custom_call" | custom-call | tf_op jit(solution)/shard_map/pallas_call | solution.py:25
  9.2 7.6 %all-to-all-start = ((s32[32,1,128]{2,1,0:T(1,128)}), s32[32,1,128]{2,1,0:T(1,128)S(1)}, u32[]{:S(2)}, u32[]{:S(2)}) async-start(s32[32,1,128]{2,1,0:T(1,128)} %bitcast.5), calls=%async_computation | async-start | bytes 32768 | tf_op jit(solution)/shard_map/all_to_all | solution.py:287
  16.8 0.9 stage.1.own_ref
  17.8 5.2 %all-to-all-done.table_ref = s32[32,1,128]{2,1,0:T(1,128)S(1)} async-done(((s32[32,1,128]{2,1,0:T(1,128)}), s32[32,1,128]{2,1,0:T(1,128)S(1)}, u32[]{:S(2)}, u32[]{:S(2)}) %all-to-all-start) | async-done | bytes 16416 | tf_op jit(solution)/shard_map/all_to_all | solution.py:287
  22.9 0.0 collective-permute-done.twin_ref
  22.9 2.7 %pack.1 = f32[32,2,2,16,256]{4,3,2,1,0:T(8,128)} custom-call(s32[32,1,128]{2,1,0:T(1,128)S(1)} %all-to-all-done.table_ref, f32[8,16,256]{2,1,0:T(8,128)S(1)} %stage.1.own_ref, f32[8,16,256]{2,1,0:T(8,128)S(1)} %collective-permute-done.twin_ref), custom_call_target="tpu_custom_call" | custom-call | tf_op jit(solution)/shard_map/pack/pallas_call | solution.py:92
  25.7 5.1 %all-to-all-start.1 = ((f32[32,2,2,16,256]{4,3,2,1,0:T(8,128)}), f32[32,2,2,16,256]{4,3,2,1,0:T(8,128)S(1)}, u32[]{:S(2)}, u32[]{:S(2)}) async-start(f32[32,2,2,16,256]{4,3,2,1,0:T(8,128)} %pack.1), calls=%async_computation.1 | async-start | bytes 4194304 | tf_op jit(solution)/shard_map/all_to_all | solution.py:287
  30.9 0.1 collective-permute-start.1
  31.0 11.3 %split_kernel.1 = (bf16[8,6,256,256]{3,2,1,0:T(8,128)(2,1)}, bf16[8,6,256,256]{3,2,1,0:T(8,128)(2,1)}) custom-call(f32[8,6,256,256]{3,2,1,0:T(8,128)} %bitcast.17), custom_call_target="tpu_custom_call" | custom-call | tf_op jit(solution)/shard_map/split_kernel/pallas_call | solution.py:113
  42.3 16.5 %all-to-all-done.1.received_ref = f32[32,2,2,16,256]{4,3,2,1,0:T(8,128)S(1)} async-done(((f32[32,2,2,16,256]{4,3,2,1,0:T(8,128)}), f32[32,2,2,16,256]{4,3,2,1,0:T(8,128)S(1)}, u32[]{:S(2)}, u32[]{:S(2)}) %all-to-all-start.1) | async-done | bytes 2097184 | tf_op jit(solution)/shard_map/all_to_all | solution.py:287
  58.8 8.6 %near.1 = (f32[8,16,256]{2,1,0:T(8,128)}, f32[16,256]{1,0:T(8,128)S(1)}) custom-call(s32[6,1,8]{2,1,0:T(1,128)S(1)} %bitcast.15, s32[3]{0:T(128)S(1)} %pad_add_fusion.place_ref, f32[32,2,2,16,256]{4,3,2,1,0:T(8,128)S(1)} %all-to-all-done.1.received_ref, bf16[8,6,256,256]{3,2,1,0:T(8,128)(2,1)} %get-tuple-element.13.high_ref, ...), custom_call_target="tpu_custom_call" | custom-call | tf_op jit(solution)/shard_map/near/pallas_call | solution.py:153
  67.4 3.4 %all-to-all-start.2 = ((f32[8,16,256]{2,1,0:T(8,128)}), f32[8,16,256]{2,1,0:T(8,128)S(1)}, u32[]{:S(2)}, u32[]{:S(2)}) async-start(f32[8,16,256]{2,1,0:T(8,128)} %get-tuple-element.15), calls=%async_computation.2 | async-start | bytes 262144 | tf_op jit(solution)/shard_map/all_to_all | solution.py:287
  70.8 0.7 slice_bitcast_fusion
  71.5 3.8 %collective-permute-start.2 = (f32[16,256]{1,0:T(8,128)S(1)}, f32[16,256]{1,0:T(8,128)S(1)}, u32[]{:S(2)}, u32[]{:S(2)}) collective-permute-start(f32[16,256]{1,0:T(8,128)S(1)} %slice_bitcast_fusion), channel_id=1, source_target_pairs={{0,1},{1,2},{2,3},{4,5},{5,6},{6,7},{8,9},{9,10},{10,11},{12,13},{... | collective-permute-start | bytes 49160 | tf_op jit(solution)/shard_map/ppermute | solution.py:295
  75.3 5.5 %collective-permute-start.3 = (f32[16,256]{1,0:T(8,128)S(1)}, f32[16,256]{1,0:T(8,128)S(1)}, u32[]{:S(2)}, u32[]{:S(2)}) collective-permute-start(f32[16,256]{1,0:T(8,128)S(1)} %slice_bitcast_fusion), channel_id=1, source_target_pairs={{0,129},{1,130},{2,131},{128,1},{129,2},{130,3},{4,133},{5,134},{6... | collective-permute-start | bytes 49160 | tf_op jit(solution)/shard_map/ppermute | solution.py:297
  80.8 0.0 collective-permute-done.2.before_ref
  80.8 1.4 %collective-permute-done.3.twin_before_ref = f32[16,256]{1,0:T(8,128)S(1)} collective-permute-done((f32[16,256]{1,0:T(8,128)S(1)}, f32[16,256]{1,0:T(8,128)S(1)}, u32[]{:S(2)}, u32[]{:S(2)}) %collective-permute-start.3) | collective-permute-done | bytes 16416 | tf_op jit(solution)/shard_map/ppermute | solution.py:297
  82.2 0.0 collective-permute-done.1.aside_ref
  82.3 0.8 shard_map.57
  83.1 14.3 %all_to_all.20.mine_ref = f32[16,2,16,256]{3,2,1,0:T(8,128)S(1)} all-to-all(f32[16,2,16,256]{3,2,1,0:T(8,128)S(1)} %get-tuple-element.19), channel_id=1, replica_groups=mesh['z_hi'=2,'y'=4,'x'=4,'core'=2,'lags'=4] {'y','x'}, dimensions={0} | all-to-all | bytes 1048576 | tf_op jit(solution)/shard_map/all_to_all | solution.py:287
  97.3 1.9 %collective-permute-done.4.partner_ref = f32[16,2,16,256]{3,2,1,0:T(8,128)S(1)} collective-permute-done((f32[16,2,16,256]{3,2,1,0:T(8,128)S(1)}, f32[16,2,16,256]{3,2,1,0:T(8,128)S(1)}, u32[]{:S(2)}, u32[]{:S(2)}) %collective-permute-start.4) | collective-permute-done | bytes 524320 | tf_op jit(solution)/shard_map/ppermute | solution.py:307
  99.3 1.7 %first_lag.1.refs_0_ = f32[16,256]{1,0:T(8,128)S(1)} custom-call(s32[6,1,8]{2,1,0:T(1,128)S(1)} %bitcast.16, s32[3]{0:T(128)S(1)} %pad_add_fusion.place_ref, f32[16,2,16,256]{3,2,1,0:T(8,128)S(1)} %all_to_all.20.mine_ref, f32[16,2,16,256]{3,2,1,0:T(8,128)S(1)} %collective-permute-done.4.partner_ref, bf16[8,6,256,256]{3,2,1,0:T(8,128)(2,1)} %get-tuple-element.13.high_ref, ...), custom_call_target="tpu_custom_call" | custom-call | tf_op jit(solution)/shard_map/first_lag/pallas_call | solution.py:231
  101.0 3.6 %collective-permute-start.5 = (f32[16,256]{1,0:T(8,128)S(1)}, f32[16,256]{1,0:T(8,128)S(1)}, u32[]{:S(2)}, u32[]{:S(2)}) collective-permute-start(f32[16,256]{1,0:T(8,128)S(1)} %first_lag.1.refs_0_), channel_id=1, source_target_pairs={{0,1},{1,2},{2,3},{3,0},{4,5},{5,6},{6,7},{7,4},{8,9},{9,10},{10,1... | collective-permute-start | bytes 49160 | tf_op jit(solution)/shard_map/ppermute | solution.py:313
  104.5 0.3 collective-permute-start.6
  104.9 2.8 %collective-permute-start.7 = (f32[16,256]{1,0:T(8,128)S(1)}, f32[16,256]{1,0:T(8,128)S(1)}, u32[]{:S(2)}, u32[]{:S(2)}) collective-permute-start(f32[16,256]{1,0:T(8,128)S(1)} %first_lag.1.refs_0_), channel_id=1, source_target_pairs={{0,3},{1,0},{2,1},{3,2},{4,7},{5,4},{6,5},{7,6},{8,11},{9,8},{10,9... | collective-permute-start | bytes 49160 | tf_op jit(solution)/shard_map/ppermute | solution.py:313
  107.7 0.0 collective-permute-done.5.refs_1_
  107.7 1.5 %collective-permute-done.6.refs_2_ = f32[16,256]{1,0:T(8,128)S(1)} collective-permute-done((f32[16,256]{1,0:T(8,128)S(1)}, f32[16,256]{1,0:T(8,128)S(1)}, u32[]{:S(2)}, u32[]{:S(2)}) %collective-permute-start.6) | collective-permute-done | bytes 16416 | tf_op jit(solution)/shard_map/ppermute | solution.py:313
  109.2 0.0 collective-permute-done.7.refs_3_
  109.2 1.3 %last_density.1 = f32[2,16,256]{2,1,0:T(8,128)} custom-call(s32[3]{0:T(128)S(1)} %pad_add_fusion.place_ref, f32[2,16,256]{2,1,0:T(8,128)S(1)} %copy-done.1, f32[256,256]{1,0:T(8,128)S(1)} %bitcast.13, f32[16,256]{1,0:T(8,128)S(1)} %get-tuple-element.18.density_ref, f32[16,256]{1,0:T(8,128)S(1)} %first_lag.1.refs_0_, ...), custom_call_target="tpu_custom_call" | custom-call | tf_op jit(solution)/shard_map/last_density/pallas_call | solution.py:264
  (12 shorter events, 0.1 us)
Async XLA Ops:
  0.0 30.8 %copy-start.1 = (f32[2,16,256]{2,1,0:T(8,128)S(1)}, f32[2,16,256]{2,1,0:T(8,128)}, u32[]{:S(2)}) copy-start(f32[2,16,256]{2,1,0:T(8,128)} %inc_ref.1) | copy-start | bytes 98308
  0.0 30.8 %copy-start = (f32[1,256,256]{2,1,0:T(8,128)S(1)}, f32[1,256,256]{2,1,0:T(8,128)}, u32[]{:S(2)}) copy-start(f32[1,256,256]{2,1,0:T(8,128)} %param.9) | copy-start | bytes 786436
  0.0 22.9 %collective-permute-start = (f32[8,16,256]{2,1,0:T(8,128)}, f32[8,16,256]{2,1,0:T(8,128)S(1)}, u32[]{:S(2)}, u32[]{:S(2)}) collective-permute-start(f32[8,16,256]{2,1,0:T(8,128)} %history_ref.1), channel_id=1, source_target_pairs={{0,128},{128,0},{1,129},{129,1},{2,130},{130,2},{3,131},{131,3},{4... | collective-permute-start | bytes 393224 | tf_op jit(solution)/shard_map/ppermute | solution.py:291
  7.3 0.7 copy-start.2
  9.2 13.7 %all-to-all-start = ((s32[32,1,128]{2,1,0:T(1,128)}), s32[32,1,128]{2,1,0:T(1,128)S(1)}, u32[]{:S(2)}, u32[]{:S(2)}) async-start(s32[32,1,128]{2,1,0:T(1,128)} %bitcast.5), calls=%async_computation | async-start | bytes 32768 | tf_op jit(solution)/shard_map/all_to_all | solution.py:287
  25.7 33.1 %all-to-all-start.1 = ((f32[32,2,2,16,256]{4,3,2,1,0:T(8,128)}), f32[32,2,2,16,256]{4,3,2,1,0:T(8,128)S(1)}, u32[]{:S(2)}, u32[]{:S(2)}) async-start(f32[32,2,2,16,256]{4,3,2,1,0:T(8,128)} %pack.1), calls=%async_computation.1 | async-start | bytes 4194304 | tf_op jit(solution)/shard_map/all_to_all | solution.py:287
  30.9 51.4 %collective-permute-start.1 = (f32[272,256]{1,0:T(8,128)S(1)}, f32[272,256]{1,0:T(8,128)S(1)}, u32[]{:S(2)}, u32[]{:S(2)}) collective-permute-start(f32[272,256]{1,0:T(8,128)S(1)} %pad_maximum_fusion), channel_id=1, source_target_pairs={{0,128},{128,0},{1,129},{129,1},{2,130},{130,2},{3,131},{131,3},{4... | collective-permute-start | bytes 835592 | tf_op jit(solution)/shard_map/ppermute | solution.py:298
  31.0 27.9 %copy-start.3 = (s32[1,8,6]{1,0,2:T(1,128)S(1)}, s32[1,8,6]{1,0,2:T(1,128)}, u32[]{:S(2)}) copy-start(s32[1,8,6]{1,0,2:T(1,128)} %param.8) | copy-start | bytes 580
  67.4 14.9 %all-to-all-start.2 = ((f32[8,16,256]{2,1,0:T(8,128)}), f32[8,16,256]{2,1,0:T(8,128)S(1)}, u32[]{:S(2)}, u32[]{:S(2)}) async-start(f32[8,16,256]{2,1,0:T(8,128)} %get-tuple-element.15), calls=%async_computation.2 | async-start | bytes 262144 | tf_op jit(solution)/shard_map/all_to_all | solution.py:287
  71.5 9.3 %collective-permute-start.2 = (f32[16,256]{1,0:T(8,128)S(1)}, f32[16,256]{1,0:T(8,128)S(1)}, u32[]{:S(2)}, u32[]{:S(2)}) collective-permute-start(f32[16,256]{1,0:T(8,128)S(1)} %slice_bitcast_fusion), channel_id=1, source_target_pairs={{0,1},{1,2},{2,3},{4,5},{5,6},{6,7},{8,9},{9,10},{10,11},{12,13},{... | collective-permute-start | bytes 49160 | tf_op jit(solution)/shard_map/ppermute | solution.py:295
  75.3 6.9 %collective-permute-start.3 = (f32[16,256]{1,0:T(8,128)S(1)}, f32[16,256]{1,0:T(8,128)S(1)}, u32[]{:S(2)}, u32[]{:S(2)}) collective-permute-start(f32[16,256]{1,0:T(8,128)S(1)} %slice_bitcast_fusion), channel_id=1, source_target_pairs={{0,129},{1,130},{2,131},{128,1},{129,2},{130,3},{4,133},{5,134},{6... | collective-permute-start | bytes 49160 | tf_op jit(solution)/shard_map/ppermute | solution.py:297
  97.3 1.9 %collective-permute-start.4 = (f32[16,2,16,256]{3,2,1,0:T(8,128)S(1)}, f32[16,2,16,256]{3,2,1,0:T(8,128)S(1)}, u32[]{:S(2)}, u32[]{:S(2)}) collective-permute-start(f32[16,2,16,256]{3,2,1,0:T(8,128)S(1)} %all_to_all.20.mine_ref), channel_id=1, source_target_pairs={{0,4},{4,0},{1,5},{5,1},{2,6},{6,2},{3,7},{7,3},{8,12},{12,8},{9,1... | collective-permute-start | bytes 1572872 | tf_op jit(solution)/shard_map/ppermute | solution.py:307
  101.0 6.7 %collective-permute-start.5 = (f32[16,256]{1,0:T(8,128)S(1)}, f32[16,256]{1,0:T(8,128)S(1)}, u32[]{:S(2)}, u32[]{:S(2)}) collective-permute-start(f32[16,256]{1,0:T(8,128)S(1)} %first_lag.1.refs_0_), channel_id=1, source_target_pairs={{0,1},{1,2},{2,3},{3,0},{4,5},{5,6},{6,7},{7,4},{8,9},{9,10},{10,1... | collective-permute-start | bytes 49160 | tf_op jit(solution)/shard_map/ppermute | solution.py:313
  104.5 4.6 %collective-permute-start.6 = (f32[16,256]{1,0:T(8,128)S(1)}, f32[16,256]{1,0:T(8,128)S(1)}, u32[]{:S(2)}, u32[]{:S(2)}) collective-permute-start(f32[16,256]{1,0:T(8,128)S(1)} %first_lag.1.refs_0_), channel_id=1, source_target_pairs={{0,2},{1,3},{2,0},{3,1},{4,6},{5,7},{6,4},{7,5},{8,10},{9,11},{10,... | collective-permute-start | bytes 49160 | tf_op jit(solution)/shard_map/ppermute | solution.py:313
  104.9 4.3 %collective-permute-start.7 = (f32[16,256]{1,0:T(8,128)S(1)}, f32[16,256]{1,0:T(8,128)S(1)}, u32[]{:S(2)}, u32[]{:S(2)}) collective-permute-start(f32[16,256]{1,0:T(8,128)S(1)} %first_lag.1.refs_0_), channel_id=1, source_target_pairs={{0,3},{1,0},{2,1},{3,2},{4,7},{5,4},{6,5},{7,6},{8,11},{9,8},{10,9... | collective-permute-start | bytes 49160 | tf_op jit(solution)/shard_map/ppermute | solution.py:313
